TPU v7x, 32 devices: a whole 2x2x4 slice. The times are simulated.
32 devices in a mesh: slab: 2 (over x), scan: 8 (over z, y), mz: 2 (over core).
Axes of the slice: x: 2, y: 2, z: 4, core: 2. Of those that a mesh axis runs over, the one named last changes fastest.
Arguments:
- spectra: bfloat16 [12288, 8192], P('mz', ('slab', 'scan')), parts along dimension 1, may hold values from 0 to 1
- templates: bfloat16 [2, 12288, 512], P('mz', ('slab', 'scan')), parts along dimension 1, may hold values from 0 to 2
- activations: float32 [64, 8192], P(None, ('slab', 'scan')), parts along dimension 1, may hold values from 0 to 1
- h_rate: float32 [64], replicated, may hold values from 0.02 to 0.08
- w_rate: float32 [64], replicated, may hold values from 0.2 to 0.8
Outputs:
- new_activations: float32 [64, 8192], P(None, ('slab', 'scan')), parts along dimension 1
- new_templates: bfloat16 [2, 12288, 512], P('mz', ('slab', 'scan')), parts along dimension 1
There are 2 independent parts, one for each index of `slab`. A program takes and returns all parts, laid end to end along the dimension named above; an argument that names none is the same for every part. Nothing has to cross between parts.
All inputs are finite; a program needn't handle non-finite values.
Results may differ from a plain program's by a relative error of at most 0.00082.
Values may be sent and summed in bfloat16 or wider, within the bound.
No kernel may reach another device: no remote copies, remote signals or barrier semaphores. Data moves between devices by JAX's collectives and lax.ppermute only.
A program may use at most 128 MiB of HBM per device.

v0:
```python
import functools

import jax
import jax.numpy as jnp
from jax import lax
from jax.experimental import pallas as pl
from jax.experimental.pallas import tpu as pltpu
from jax.sharding import PartitionSpec as P


LAG = 64
PAIR = 2 * LAG

SWAP = [(0, 1), (1, 0)]

VMEM = pl.BlockSpec(memory_space=pltpu.VMEM)
SMEM = pl.BlockSpec(memory_space=pltpu.SMEM)
ANY = pl.BlockSpec(memory_space=pl.ANY)


def aligned(start):
    return pl.multiple_of(start, PAIR)


def fill_stack(core, place, mine, other, pairs, pad):
    blocks, comps, half = mine.shape
    width = 2 * half
    pairs[:, :pad] = jnp.zeros((2 * comps, pad), pairs.dtype)

    def put(first, second):
        def one(e, _):
            at = pad + place(e) * width
            pairs[:comps, pl.ds(aligned(at), half)] = first[e]
            pairs[:comps, pl.ds(aligned(at + half), half)] = second[e]
            return 0

        lax.fori_loop(0, blocks, one, 0)

    @pl.when(core == 0)
    def _():
        put(mine, other)

    @pl.when(core == 1)
    def _():
        put(other, mine)

    def shift(b, _):
        at = pad + b * width
        wide = pairs[:comps, pl.ds(aligned(at - PAIR), width + PAIR)]
        pairs[comps:, pl.ds(aligned(at), width)] = wide[:, PAIR - LAG : PAIR - LAG + width]
        return 0

    lax.fori_loop(0, blocks, shift, 0)


def lagged_tile(pairs, start, width, count):
    return jnp.concatenate(
        [pairs[:, pl.ds(aligned(start - p * PAIR), width)] for p in range(count)], 0
    )


def stack_kernel(pad, core, ids, mine, other, pairs):
    fill_stack(core[0], lambda e: ids[e], mine, other, pairs, pad)


def first_kernel(scale, pad, chained, core, ids, w, wt, pairs, *rest):
    before, rest = rest[: 2 * chained], rest[2 * chained :]
    datas, (give, keep, total, resid) = rest[:-4], rest[-4:]
    lagrows = w.shape[1]
    _, comps, half = give.shape
    _, width = datas[0].shape
    count = lagrows // (2 * comps)
    lead = total.shape[1] - width - PAIR
    if chained:
        give[...] = before[0][...]
        keep[...] = before[1][...]
    else:
        give[...] = jnp.zeros_like(give)
        keep[...] = jnp.zeros_like(keep)

    for i, data in enumerate(datas):
        source = ids[i]
        stack = lagged_tile(pairs, pad + source * width, width, count)
        recon = jnp.dot(w[...], stack, preferred_element_type=jnp.float32)
        resid[...] = (scale * recon - data[...].astype(jnp.float32)).astype(jnp.bfloat16)
        total[...] = jnp.zeros_like(total)
        prods = jnp.dot(wt[...], resid[...], preferred_element_type=jnp.float32)
        for p in range(count):
            at = lead - p * PAIR
            total[:, at : at + width] += prods[p * 2 * comps : (p + 1) * 2 * comps]
        back = lead // width
        for q in range(back + 1):
            block = source - back + q

            def fold(outs, q=q, block=block):
                for h in range(2):
                    start = q * width + h * half
                    outs[h][block] += (
                        total[:comps, start : start + half]
                        + total[comps:, start + LAG : start + LAG + half]
                    )

            @pl.when((block >= 0) & (core[0] == 0))
            def _():
                fold((keep, give))

            @pl.when((block >= 0) & (core[0] == 1))
            def _():
                fold((give, keep))


def second_kernel(scale, pad, core, ids, w, rate, mine, other, *rest):
    blocks, comps, half = mine.shape
    width = 2 * half
    datas, (out, pairs, total, held, sems) = rest[:blocks], rest[blocks:]
    _, lagrows = w.shape
    count = lagrows // (2 * comps)
    copies = [pltpu.make_async_copy(d, held.at[i], sems.at[i]) for i, d in enumerate(datas)]
    for copy in copies:
        copy.start()
    fill_stack(core[0], lambda e: e, mine, other, pairs, pad)
    total[...] = jnp.zeros_like(total)

    def one(i, _):
        pltpu.make_async_copy(held.at[i], held.at[i], sems.at[i]).wait()
        stack = lagged_tile(pairs, pad + ids[i] * width, width, count)
        recon = jnp.dot(w[...], stack, preferred_element_type=jnp.float32)
        resid = (scale * recon - held[i].astype(jnp.float32)).astype(jnp.bfloat16)
        total[...] += lax.dot_general(
            resid, stack, (((1,), (1,)), ((), ())), preferred_element_type=jnp.float32
        )
        return 0

    lax.fori_loop(0, blocks, one, 0)
    rates = jnp.concatenate([rate[...]] * (lagrows // comps), 1)
    out[...] = jnp.maximum(
        w[...].astype(jnp.float32) - rates * (scale * total[...]), 0.0
    ).astype(jnp.bfloat16)


def cost(rows, lagrows, scans):
    return pl.CostEstimate(
        flops=4 * rows * lagrows * scans, bytes_accessed=2 * rows * scans, transcendentals=0
    )


def send_order(count):
    far = list(range(count // 2, count))
    near = list(range(2, count // 2)) + [1]
    order = []
    while far or near:
        order += far[:1] + near[:1]
        far, near = far[1:], near[1:]
    return order


def sent(x, count, k):
    return lax.ppermute(x, "scan", [(i, i ^ k) for i in range(count)])


def gathered(x, count):
    copies = jnp.broadcast_to(x[None], (count,) + x.shape)
    return lax.all_to_all(copies, "scan", 0, 0, tiled=True)


def per_device(spectra, templates, activations, h_rate, w_rate):
    count = lax.axis_size("scan")
    me = lax.axis_index("scan").astype(jnp.int32)
    core = lax.axis_index("mz").astype(jnp.int32)
    rows, lagrows = templates.shape[1:]
    comps, width = activations.shape
    half = width // 2
    scale = 1.0 / lagrows
    lags = lagrows // comps
    pad = -(-lags * LAG // PAIR) * PAIR
    lead = -(-pad // width) * width
    core_id = core[None]

    def ids(ks):
        return me ^ jnp.array(ks, jnp.int32)

    own = templates.reshape(rows, lagrows)
    own_t = own.T
    act_half = lax.dynamic_slice(activations, (0, core * half), (comps, half))

    rounded = act_half.astype(jnp.bfloat16)
    even = list(range(0, count, 2))
    blocks = spectra.reshape(count, rows, width)
    order = send_order(count)
    landed = {}
    block = rounded
    for i, k in enumerate(order + [0]):
        place, block, rounded = lax.optimization_barrier((me ^ k, block, rounded))
        if i:
            landed[order[i - 1]] = sent(block, count, order[i - 1])
        if i == 1:
            column = jnp.stack([rounded] + [sent(rounded, count, e) for e in even[1:]])
        block = lax.dynamic_index_in_dim(blocks, place, 0, keepdims=False)
    landed[0] = block
    beside = sent(column, count, 1)

    mine = jnp.concatenate([column, beside], 0)
    other = lax.ppermute(mine, "mz", SWAP)
    stack_shape = (2 * comps, pad + count * width)
    pairs = pl.pallas_call(
        functools.partial(stack_kernel, pad),
        out_shape=jax.ShapeDtypeStruct(stack_shape, jnp.bfloat16),
        in_specs=[SMEM, SMEM, VMEM, VMEM],
        out_specs=VMEM,
        compiler_params=pltpu.CompilerParams(vmem_limit_bytes=8 << 20),
        name="stack",
    )(core_id, ids(even + [k + 1 for k in even]), mine, other)

    part = (count, comps, half)
    group = max(2, count // 4)
    groups = [order[i : i + group] for i in range(0, count - 2, group)] + [order[-1:]]
    groups[0] = [0] + groups[0]
    sums = ()
    for ks in groups:
        sums = pl.pallas_call(
            functools.partial(first_kernel, scale, pad, bool(sums)),
            out_shape=[jax.ShapeDtypeStruct(part, jnp.float32)] * 2,
            in_specs=[SMEM, SMEM] + [VMEM] * (3 + len(sums) + len(ks)),
            out_specs=[VMEM] * 2,
            scratch_shapes=[
                pltpu.VMEM((2 * comps, lead + width + PAIR), jnp.float32),
                pltpu.VMEM((rows, width), jnp.bfloat16),
            ],
            cost_estimate=cost(rows, lagrows, width * len(ks)),
            compiler_params=pltpu.CompilerParams(vmem_limit_bytes=24 << 20),
            name="first",
        )(core_id, ids(ks), own, own_t, pairs, *sums, *[landed[k] for k in ks])

    give, keep = sums
    both = keep + lax.ppermute(give, "mz", SWAP)
    pieces = lax.all_to_all(both, "scan", 0, 0, tiled=True)
    grad = scale * jnp.sum(pieces, 0)
    new_half = jnp.maximum(act_half - h_rate[:, None] * grad, 0.0)
    mine_new = gathered(new_half.astype(jnp.bfloat16), count)
    other_new = lax.ppermute(mine_new, "mz", SWAP)
    new_other = lax.ppermute(new_half, "mz", SWAP)
    new_h = jnp.where(
        core == 0,
        jnp.concatenate([new_half, new_other], 1),
        jnp.concatenate([new_other, new_half], 1),
    )

    new_w = pl.pallas_call(
        functools.partial(second_kernel, scale, pad),
        out_shape=jax.ShapeDtypeStruct((rows, lagrows), jnp.bfloat16),
        in_specs=[SMEM, SMEM] + [VMEM] * 4 + [ANY] * count,
        out_specs=VMEM,
        scratch_shapes=[
            pltpu.VMEM(stack_shape, jnp.bfloat16),
            pltpu.VMEM((rows, lagrows), jnp.float32),
            pltpu.VMEM((count, rows, width), jnp.bfloat16),
            pltpu.SemaphoreType.DMA((count,)),
        ],
        cost_estimate=cost(rows, lagrows, width * count),
        compiler_params=pltpu.CompilerParams(vmem_limit_bytes=32 << 20),
        name="second",
    )(
        core_id,
        ids([0] + order),
        own,
        w_rate[None, :],
        mine_new,
        other_new,
        *[landed[k] for k in [0] + order],
    )
    return (new_h, new_w.reshape(templates.shape))


def solution(mesh):
    placed = (
        P("mz", ("slab", "scan")),
        P("mz", ("slab", "scan"), None),
        P(None, ("slab", "scan")),
        P(),
        P(),
    )

    return jax.shard_map(
        per_device,
        mesh=mesh,
        in_specs=placed,
        out_specs=(P(None, ("slab", "scan")), P("mz", ("slab", "scan"), None)),
        check_vma=False,
    )
```

profile of v0, /device:TPU:0, one launch (start us, length us, event | category | flops | bytes accessed | tf_op | source)
XLA Modules:
  0.0 201.4 jit_solution(11266122216126678370)
XLA Ops:
  0.6 0.0 copy-start.15
  0.6 0.0 copy-start.14
  0.7 0.0 copy-start.13
  0.7 0.9 dynamic-slice_convert_fusion
  1.5 2.1 %dynamic-slice_bitcast_fusion.7 = bf16[768,512]{1,0:T(8,128)(2,1)} fusion(bf16[8,768,512]{2,1,0:T(8,128)(2,1)} %bitcast.39, s32[]{:T(128)S(6)} %select_n.38), kind=kLoop, calls=%fused_computation.7 | loop fusion | bytes 1572868 | tf_op jit(solution)/shard_map/jit(dynamic_index_in_dim)/squeeze | solution.py:198
  3.6 3.1 %collective-permute-start = (bf16[64,256]{1,0:T(8,128)(2,1)S(1)}, bf16[64,256]{1,0:T(8,128)(2,1)S(1)}, u32[]{:S(2)}, u32[]{:S(2)}) collective-permute-start(bf16[64,256]{1,0:T(8,128)(2,1)S(1)} %dynamic-slice_convert_fusion), channel_id=1, source_target_pairs={{0,4},{2,6},{4,0},{6,2},{8,12},{10,14},{12,8},{14,10},{1,5},{3,7},... | collective-permute-start | bytes 98312 | tf_op jit(solution)/shard_map/ppermute | solution.py:158
  6.6 2.6 %collective-permute-start.1 = (bf16[64,256]{1,0:T(8,128)(2,1)S(1)}, bf16[64,256]{1,0:T(8,128)(2,1)S(1)}, u32[]{:S(2)}, u32[]{:S(2)}) collective-permute-start(bf16[64,256]{1,0:T(8,128)(2,1)S(1)} %dynamic-slice_convert_fusion), channel_id=1, source_target_pairs={{0,8},{2,10},{4,12},{6,14},{8,0},{10,2},{12,4},{14,6},{1,9},{3,11}... | collective-permute-start | bytes 98312 | tf_op jit(solution)/shard_map/ppermute | solution.py:158
  9.2 0.0 collective-permute-start.2
  9.2 2.1 %dynamic-slice_bitcast_fusion.6 = bf16[768,512]{1,0:T(8,128)(2,1)} fusion(bf16[8,768,512]{2,1,0:T(8,128)(2,1)} %bitcast.40, s32[]{:T(128)S(6)} %select_n.39), kind=kLoop, calls=%fused_computation.6 | loop fusion | bytes 1572868 | tf_op jit(solution)/shard_map/jit(dynamic_index_in_dim)/squeeze | solution.py:198
  11.3 0.9 collective-permute-start.6
  12.2 3.5 %collective-permute-start.5 = (bf16[768,512]{1,0:T(8,128)(2,1)}, bf16[768,512]{1,0:T(8,128)(2,1)S(1)}, u32[]{:S(2)}, u32[]{:S(2)}) collective-permute-start(bf16[768,512]{1,0:T(8,128)(2,1)} %dynamic-slice_bitcast_fusion.7), channel_id=1, source_target_pairs={{0,8},{2,10},{4,12},{6,14},{8,0},{10,2},{12,4},{14,6},{1,9},{3,11}... | collective-permute-start | bytes 2359304 | tf_op jit(solution)/shard_map/ppermute | solution.py:158
  15.7 2.1 %dynamic-slice_bitcast_fusion.5 = bf16[768,512]{1,0:T(8,128)(2,1)} fusion(bf16[8,768,512]{2,1,0:T(8,128)(2,1)} %bitcast.41, s32[]{:T(128)S(6)} %select_n.40), kind=kLoop, calls=%fused_computation.5 | loop fusion | bytes 1572868 | tf_op jit(solution)/shard_map/jit(dynamic_index_in_dim)/squeeze | solution.py:198
  17.7 2.1 %dynamic-slice_bitcast_fusion.4 = bf16[768,512]{1,0:T(8,128)(2,1)} fusion(bf16[8,768,512]{2,1,0:T(8,128)(2,1)} %bitcast.42, s32[]{:T(128)S(6)} %select_n.41), kind=kLoop, calls=%fused_computation.4 | loop fusion | bytes 1572868 | tf_op jit(solution)/shard_map/jit(dynamic_index_in_dim)/squeeze | solution.py:198
  19.9 2.1 %dynamic-slice_bitcast_fusion.3 = bf16[768,512]{1,0:T(8,128)(2,1)} fusion(bf16[8,768,512]{2,1,0:T(8,128)(2,1)} %bitcast.43, s32[]{:T(128)S(6)} %select_n.42), kind=kLoop, calls=%fused_computation.3 | loop fusion | bytes 1572868 | tf_op jit(solution)/shard_map/jit(dynamic_index_in_dim)/squeeze | solution.py:198
  21.9 0.0 collective-permute-done
  21.9 1.0 collective-permute-start.8
  22.9 0.5 collective-permute-start.7
  23.4 0.0 collective-permute-done.2
  23.4 1.8 collective-permute-start.3
  25.3 3.2 %collective-permute-done.3 = bf16[4,64,256]{2,1,0:T(8,128)(2,1)S(1)} collective-permute-done((bf16[4,64,256]{2,1,0:T(8,128)(2,1)S(1)}, bf16[4,64,256]{2,1,0:T(8,128)(2,1)S(1)}, u32[]{:S(2)}, u32[]{:S(2)}) %collective-permute-start.3) | collective-permute-done | bytes 131104 | tf_op jit(solution)/shard_map/ppermute | solution.py:158
  28.5 0.1 collective-permute-start.4
  28.6 2.1 %dynamic-slice_bitcast_fusion.2 = bf16[768,512]{1,0:T(8,128)(2,1)} fusion(bf16[8,768,512]{2,1,0:T(8,128)(2,1)} %bitcast.44, s32[]{:T(128)S(6)} %select_n.43), kind=kLoop, calls=%fused_computation.2 | loop fusion | bytes 1572868 | tf_op jit(solution)/shard_map/jit(dynamic_index_in_dim)/squeeze | solution.py:198
  30.7 1.7 collective-permute-start.10
  32.4 17.4 %collective-permute-done.6.rest_2_ = bf16[768,512]{1,0:T(8,128)(2,1)S(1)} collective-permute-done((bf16[768,512]{1,0:T(8,128)(2,1)}, bf16[768,512]{1,0:T(8,128)(2,1)S(1)}, u32[]{:S(2)}, u32[]{:S(2)}) %collective-permute-start.6) | collective-permute-done | bytes 786464 | tf_op jit(solution)/shard_map/ppermute | solution.py:158
  49.9 1.7 collective-permute-start.9
  51.6 2.1 %dynamic-slice_bitcast_fusion.1 = bf16[768,512]{1,0:T(8,128)(2,1)} fusion(bf16[8,768,512]{2,1,0:T(8,128)(2,1)} %bitcast.45, s32[]{:T(128)S(6)} %select_n.44), kind=kLoop, calls=%fused_computation.1 | loop fusion | bytes 1572868 | tf_op jit(solution)/shard_map/jit(dynamic_index_in_dim)/squeeze | solution.py:198
  53.7 0.0 collective-permute-done.5.rest_1_
  53.7 0.9 copy-done.6
  54.6 3.5 %collective-permute-start.11 = (bf16[768,512]{1,0:T(8,128)(2,1)}, bf16[768,512]{1,0:T(8,128)(2,1)S(1)}, u32[]{:S(2)}, u32[]{:S(2)}) collective-permute-start(bf16[768,512]{1,0:T(8,128)(2,1)} %dynamic-slice_bitcast_fusion.1), channel_id=1, source_target_pairs={{0,14},{2,12},{4,10},{6,8},{8,6},{10,4},{12,2},{14,0},{1,15},{3,13... | collective-permute-start | bytes 2359304 | tf_op jit(solution)/shard_map/ppermute | solution.py:158
  58.1 1.2 dynamic-slice_bitcast_fusion.rest_0_
  59.3 0.3 copy.16.wt
  59.6 0.9 copy-done.2
  60.5 1.4 stack.21.pairs
  61.9 1.1 copy-done.4
  63.1 1.1 copy-done.7
  64.2 4.2 %first.4 = (f32[8,64,256]{2,1,0:T(8,128)S(1)}, f32[8,64,256]{2,1,0:T(8,128)S(1)}) custom-call(s32[1]{0:T(128)} %bitcast.core, s32[3]{0:T(128)S(1)} %broadcast_xor_fusion.ids, bf16[768,512]{1,0:T(8,128)(2,1)S(1)} %bitcast.33, bf16[512,768]{1,0:T(8,128)(2,1)S(1)} %copy.16.wt, bf16[128,4608]{1,0:T(8,128)(2,1)S(1)} %stack.21.pairs, ...), custom_call_target="tpu_custom_call" | custom-call | flops 2415919104 | bytes 2359296 | tf_op jit(solution)/shard_map/first/pallas_call | solution.py:220
  68.3 12.8 %collective-permute-done.8.rest_3_.rest_4_ = bf16[768,512]{1,0:T(8,128)(2,1)} collective-permute-done((bf16[768,512]{1,0:T(8,128)(2,1)}, bf16[768,512]{1,0:T(8,128)(2,1)}, u32[]{:S(2)}, u32[]{:S(2)}) %collective-permute-start.8) | collective-permute-done | bytes 786464 | tf_op jit(solution)/shard_map/ppermute | solution.py:158
  81.2 38.5 %collective-permute-done.7.rest_2_.rest_3_ = bf16[768,512]{1,0:T(8,128)(2,1)} collective-permute-done((bf16[768,512]{1,0:T(8,128)(2,1)}, bf16[768,512]{1,0:T(8,128)(2,1)}, u32[]{:S(2)}, u32[]{:S(2)}) %collective-permute-start.7) | collective-permute-done | bytes 786464 | tf_op jit(solution)/shard_map/ppermute | solution.py:158
  119.7 3.9 %first.5 = (f32[8,64,256]{2,1,0:T(8,128)S(1)}, f32[8,64,256]{2,1,0:T(8,128)S(1)}) custom-call(s32[1]{0:T(128)} %bitcast.core, s32[2]{0:T(128)S(1)} %broadcast_xor_fusion.1.ids, bf16[768,512]{1,0:T(8,128)(2,1)S(1)} %bitcast.34, bf16[512,768]{1,0:T(8,128)(2,1)S(1)} %copy.16.wt, bf16[128,4608]{1,0:T(8,128)(2,1)S(1)} %stack.21.pairs, ...), custom_call_target="tpu_custom_call" | custom-call | flops 1610612736 | bytes 1572864 | tf_op jit(solution)/shard_map/first/pallas_call | solution.py:220
  123.6 0.0 collective-permute-done.10.rest_3_.rest_6_
  123.6 0.0 collective-permute-done.9.rest_2_.rest_5_
  123.6 0.0 copy-start.11
  123.6 0.0 copy-start.10
  123.7 0.0 copy-start.9
  123.7 4.0 %first.6 = (f32[8,64,256]{2,1,0:T(8,128)S(1)}, f32[8,64,256]{2,1,0:T(8,128)S(1)}) custom-call(s32[1]{0:T(128)} %bitcast.core, s32[2]{0:T(128)S(1)} %broadcast_xor_fusion.2.ids, bf16[768,512]{1,0:T(8,128)(2,1)S(1)} %bitcast.35, bf16[512,768]{1,0:T(8,128)(2,1)S(1)} %copy.16.wt, bf16[128,4608]{1,0:T(8,128)(2,1)S(1)} %stack.21.pairs, ...), custom_call_target="tpu_custom_call" | custom-call | flops 1610612736 | bytes 1572864 | tf_op jit(solution)/shard_map/first/pallas_call | solution.py:220
  127.7 0.0 collective-permute-done.11.rest_2_.rest_7_
  127.7 1.3 first.7
  129.0 0.1 collective-permute-start.12
  129.1 1.9 collective-permute-done.12
  131.0 0.9 add.40
  131.8 26.4 %all-to-all-start = ((f32[8,64,256]{2,1,0:T(8,128)}), f32[8,64,256]{2,1,0:T(8,128)S(1)}, u32[]{:S(2)}, u32[]{:S(2)}) async-start(f32[8,64,256]{2,1,0:T(8,128)} %add.40), calls=%async_computation | async-start | bytes 1048576 | tf_op jit(solution)/shard_map/all_to_all | solution.py:236
  158.2 14.8 %all-to-all-done = f32[8,64,256]{2,1,0:T(8,128)S(1)} async-done(((f32[8,64,256]{2,1,0:T(8,128)}), f32[8,64,256]{2,1,0:T(8,128)S(1)}, u32[]{:S(2)}, u32[]{:S(2)}) %all-to-all-start) | async-done | bytes 524320 | tf_op jit(solution)/shard_map/all_to_all | solution.py:236
  173.1 0.1 fusion
  173.1 0.7 broadcast_in_dim.15
  173.9 3.6 %all-to-all-start.1 = ((bf16[8,64,256]{2,1,0:T(8,128)(2,1)}), bf16[8,64,256]{2,1,0:T(8,128)(2,1)S(1)}, u32[]{:S(2)}, u32[]{:S(2)}) async-start(bf16[8,64,256]{2,1,0:T(8,128)(2,1)} %broadcast_in_dim.15), calls=%async_computation.1 | async-start | bytes 524288 | tf_op jit(solution)/shard_map/all_to_all | solution.py:163
  177.5 0.0 collective-permute-start.13
  177.5 9.1 %all-to-all-done.1.mine = bf16[8,64,256]{2,1,0:T(8,128)(2,1)S(1)} async-done(((bf16[8,64,256]{2,1,0:T(8,128)(2,1)}), bf16[8,64,256]{2,1,0:T(8,128)(2,1)S(1)}, u32[]{:S(2)}, u32[]{:S(2)}) %all-to-all-start.1) | async-done | bytes 262176 | tf_op jit(solution)/shard_map/all_to_all | solution.py:163
  186.6 0.0 collective-permute-start.14
  186.6 0.7 broadcast_xor_fusion.3.ids
  187.3 0.7 maximum_select_fusion
  187.9 0.2 collective-permute-done.14.other
  188.1 1.1 copy-done.5
  189.3 1.1 copy-done.8
  190.4 11.0 %second.1 = bf16[768,512]{1,0:T(8,128)(2,1)} custom-call(s32[1]{0:T(128)} %bitcast.core, s32[8]{0:T(128)S(1)} %broadcast_xor_fusion.3.ids, bf16[768,512]{1,0:T(8,128)(2,1)S(1)} %bitcast.37, f32[1,64]{1,0:T(1,128)S(1)} %bitcast.38, bf16[8,64,256]{2,1,0:T(8,128)(2,1)S(1)} %all-to-all-done.1.mine, bf16[8,64,256]{2,1,0:T(8,128)(2,1)S(1)} %collective-permute-done.14.other, ...), custom_call_target="tpu_custom_call" | custom-call | flops 6442450944 | bytes 6291456 | tf_op jit(solution)/shard_map/second/pallas_call | solution.py:248
  (35 shorter events, 0.1 us)
Async XLA Ops:
  0.6 19.2 %copy-start.15 = (s32[8]{0:T(128)S(1)}, s32[8]{0:T(128)}, u32[]{:S(2)}) copy-start(s32[8]{0:T(128)} %constant.64.clone) | copy-start | bytes 100
  0.6 19.2 %copy-start.14 = (s32[3]{0:T(128)S(1)}, s32[3]{0:T(128)}, u32[]{:S(2)}) copy-start(s32[3]{0:T(128)} %constant.65.clone) | copy-start | bytes 40
  0.7 27.9 %copy-start.13 = (s32[2]{0:T(128)S(1)}, s32[2]{0:T(128)}, u32[]{:S(2)}) copy-start(s32[2]{0:T(128)} %constant.66.clone) | copy-start | bytes 28
  3.6 55.7 %copy-start = (bf16[1,768,512]{2,1,0:T(8,128)(2,1)S(1)}, bf16[1,768,512]{2,1,0:T(8,128)(2,1)}, u32[]{:S(2)}) copy-start(bf16[1,768,512]{2,1,0:T(8,128)(2,1)} %param.12) | copy-start | bytes 2359300
  3.6 18.4 %collective-permute-start = (bf16[64,256]{1,0:T(8,128)(2,1)S(1)}, bf16[64,256]{1,0:T(8,128)(2,1)S(1)}, u32[]{:S(2)}, u32[]{:S(2)}) collective-permute-start(bf16[64,256]{1,0:T(8,128)(2,1)S(1)} %dynamic-slice_convert_fusion), channel_id=1, source_target_pairs={{0,4},{2,6},{4,0},{6,2},{8,12},{10,14},{12,8},{14,10},{1,5},{3,7},... | collective-permute-start | bytes 98312 | tf_op jit(solution)/shard_map/ppermute | solution.py:158
  6.6 16.3 %collective-permute-start.1 = (bf16[64,256]{1,0:T(8,128)(2,1)S(1)}, bf16[64,256]{1,0:T(8,128)(2,1)S(1)}, u32[]{:S(2)}, u32[]{:S(2)}) collective-permute-start(bf16[64,256]{1,0:T(8,128)(2,1)S(1)} %dynamic-slice_convert_fusion), channel_id=1, source_target_pairs={{0,8},{2,10},{4,12},{6,14},{8,0},{10,2},{12,4},{14,6},{1,9},{3,11}... | collective-permute-start | bytes 98312 | tf_op jit(solution)/shard_map/ppermute | solution.py:158
  9.2 14.2 %collective-permute-start.2 = (bf16[64,256]{1,0:T(8,128)(2,1)S(1)}, bf16[64,256]{1,0:T(8,128)(2,1)S(1)}, u32[]{:S(2)}, u32[]{:S(2)}) collective-permute-start(bf16[64,256]{1,0:T(8,128)(2,1)S(1)} %dynamic-slice_convert_fusion), channel_id=1, source_target_pairs={{0,12},{2,14},{4,8},{6,10},{8,4},{10,6},{12,0},{14,2},{1,13},{3,15... | collective-permute-start | bytes 98312 | tf_op jit(solution)/shard_map/ppermute | solution.py:158
  11.3 48.3 %copy-start.12 = (s32[2]{0:T(128)S(1)}, s32[2]{0:T(128)}, u32[]{:S(2)}) copy-start(s32[2]{0:T(128)} %constant.67.clone) | copy-start | bytes 28
  11.3 38.5 %collective-permute-start.6 = (bf16[768,512]{1,0:T(8,128)(2,1)}, bf16[768,512]{1,0:T(8,128)(2,1)S(1)}, u32[]{:S(2)}, u32[]{:S(2)}) collective-permute-start(bf16[768,512]{1,0:T(8,128)(2,1)} %dynamic-slice_bitcast_fusion.6), channel_id=1, source_target_pairs={{0,4},{2,6},{4,0},{6,2},{8,12},{10,14},{12,8},{14,10},{1,5},{3,7},... | collective-permute-start | bytes 2359304 | tf_op jit(solution)/shard_map/ppermute | solution.py:158
  12.2 41.5 %collective-permute-start.5 = (bf16[768,512]{1,0:T(8,128)(2,1)}, bf16[768,512]{1,0:T(8,128)(2,1)S(1)}, u32[]{:S(2)}, u32[]{:S(2)}) collective-permute-start(bf16[768,512]{1,0:T(8,128)(2,1)} %dynamic-slice_bitcast_fusion.7), channel_id=1, source_target_pairs={{0,8},{2,10},{4,12},{6,14},{8,0},{10,2},{12,4},{14,6},{1,9},{3,11}... | collective-permute-start | bytes 2359304 | tf_op jit(solution)/shard_map/ppermute | solution.py:158
  21.9 59.3 %collective-permute-start.8 = (bf16[768,512]{1,0:T(8,128)(2,1)}, bf16[768,512]{1,0:T(8,128)(2,1)}, u32[]{:S(2)}, u32[]{:S(2)}) collective-permute-start(bf16[768,512]{1,0:T(8,128)(2,1)} %dynamic-slice_bitcast_fusion.4), channel_id=1, source_target_pairs={{0,6},{2,4},{4,2},{6,0},{8,14},{10,12},{12,10},{14,8},{1,7},{3,5},... | collective-permute-start | bytes 2359304 | tf_op jit(solution)/shard_map/ppermute | solution.py:158
  22.9 96.8 %collective-permute-start.7 = (bf16[768,512]{1,0:T(8,128)(2,1)}, bf16[768,512]{1,0:T(8,128)(2,1)}, u32[]{:S(2)}, u32[]{:S(2)}) collective-permute-start(bf16[768,512]{1,0:T(8,128)(2,1)} %dynamic-slice_bitcast_fusion.5), channel_id=1, source_target_pairs={{0,10},{2,8},{4,14},{6,12},{8,2},{10,0},{12,6},{14,4},{1,11},{3,9}... | collective-permute-start | bytes 2359304 | tf_op jit(solution)/shard_map/ppermute | solution.py:158
  23.4 5.0 %collective-permute-start.3 = (bf16[4,64,256]{2,1,0:T(8,128)(2,1)S(1)}, bf16[4,64,256]{2,1,0:T(8,128)(2,1)S(1)}, u32[]{:S(2)}, u32[]{:S(2)}) collective-permute-start(bf16[4,64,256]{2,1,0:T(8,128)(2,1)S(1)} %pad_maximum_fusion), channel_id=1, source_target_pairs={{0,2},{2,0},{4,6},{6,4},{8,10},{10,8},{12,14},{14,12},{1,3},{3,1},... | collective-permute-start | bytes 393224 | tf_op jit(solution)/shard_map/ppermute | solution.py:158
  28.5 2.2 %collective-permute-start.4 = (bf16[8,64,256]{2,1,0:T(8,128)(2,1)S(1)}, bf16[8,64,256]{2,1,0:T(8,128)(2,1)S(1)}, u32[]{:S(2)}, u32[]{:S(2)}) collective-permute-start(bf16[8,64,256]{2,1,0:T(8,128)(2,1)S(1)} %constant_dynamic-update-slice_fusion.mine), channel_id=1, source_target_pairs={{0,1},{1,0},{2,3},{3,2},{4,5},{5,4},{6,7},{7,6},{8,9},{9,8},{10,11... | collective-permute-start | bytes 786440 | tf_op jit(solution)/shard_map/ppermute | solution.py:203
  30.7 28.6 %copy-start.1 = (bf16[8,64,256]{2,1,0:T(8,128)(2,1)}, bf16[8,64,256]{2,1,0:T(8,128)(2,1)S(1)}, u32[]{:S(2)}) copy-start(bf16[8,64,256]{2,1,0:T(8,128)(2,1)S(1)} %collective-permute-done.4.other) | copy-start | bytes 786436
  30.7 92.9 %collective-permute-start.10 = (bf16[768,512]{1,0:T(8,128)(2,1)}, bf16[768,512]{1,0:T(8,128)(2,1)}, u32[]{:S(2)}, u32[]{:S(2)}) collective-permute-start(bf16[768,512]{1,0:T(8,128)(2,1)} %dynamic-slice_bitcast_fusion.2), channel_id=1, source_target_pairs={{0,2},{2,0},{4,6},{6,4},{8,10},{10,8},{12,14},{14,12},{1,3},{3,1},... | collective-permute-start | bytes 2359304 | tf_op jit(solution)/shard_map/ppermute | solution.py:158
  49.9 3.8 %copy-start.3 = (bf16[768,512]{1,0:T(8,128)(2,1)}, bf16[768,512]{1,0:T(8,128)(2,1)S(1)}, u32[]{:S(2)}) copy-start(bf16[768,512]{1,0:T(8,128)(2,1)S(1)} %collective-permute-done.6.rest_2_) | copy-start | bytes 2359300
  49.9 73.8 %collective-permute-start.9 = (bf16[768,512]{1,0:T(8,128)(2,1)}, bf16[768,512]{1,0:T(8,128)(2,1)}, u32[]{:S(2)}, u32[]{:S(2)}) collective-permute-start(bf16[768,512]{1,0:T(8,128)(2,1)} %dynamic-slice_bitcast_fusion.3), channel_id=1, source_target_pairs={{0,12},{2,14},{4,8},{6,10},{8,4},{10,6},{12,0},{14,2},{1,13},{3,15... | collective-permute-start | bytes 2359304 | tf_op jit(solution)/shard_map/ppermute | solution.py:158
  53.7 0.9 copy-start.6
  54.6 73.1 %collective-permute-start.11 = (bf16[768,512]{1,0:T(8,128)(2,1)}, bf16[768,512]{1,0:T(8,128)(2,1)S(1)}, u32[]{:S(2)}, u32[]{:S(2)}) collective-permute-start(bf16[768,512]{1,0:T(8,128)(2,1)} %dynamic-slice_bitcast_fusion.1), channel_id=1, source_target_pairs={{0,14},{2,12},{4,10},{6,8},{8,6},{10,4},{12,2},{14,0},{1,15},{3,13... | collective-permute-start | bytes 2359304 | tf_op jit(solution)/shard_map/ppermute | solution.py:158
  59.6 1.0 copy-start.2
  61.9 1.1 copy-start.4
  63.1 1.1 copy-start.7
  123.6 34.6 %copy-start.11 = (f32[64]{0:T(128)S(1)}, f32[64]{0:T(128)}, u32[]{:S(2)}) copy-start(f32[64]{0:T(128)} %param.14) | copy-start | bytes 772
  123.6 49.4 %copy-start.10 = (f32[64,512]{1,0:T(8,128)S(1)}, f32[64,512]{1,0:T(8,128)}, u32[]{:S(2)}) copy-start(f32[64,512]{1,0:T(8,128)} %param.13) | copy-start | bytes 393220
  123.7 64.5 %copy-start.9 = (f32[64]{0:T(128)S(1)}, f32[64]{0:T(128)}, u32[]{:S(2)}) copy-start(f32[64]{0:T(128)} %param.15) | copy-start | bytes 772
  129.0 2.0 collective-permute-start.12
  131.8 41.2 %all-to-all-start = ((f32[8,64,256]{2,1,0:T(8,128)}), f32[8,64,256]{2,1,0:T(8,128)S(1)}, u32[]{:S(2)}, u32[]{:S(2)}) async-start(f32[8,64,256]{2,1,0:T(8,128)} %add.40), calls=%async_computation | async-start | bytes 1048576 | tf_op jit(solution)/shard_map/all_to_all | solution.py:236
  173.9 12.7 %all-to-all-start.1 = ((bf16[8,64,256]{2,1,0:T(8,128)(2,1)}), bf16[8,64,256]{2,1,0:T(8,128)(2,1)S(1)}, u32[]{:S(2)}, u32[]{:S(2)}) async-start(bf16[8,64,256]{2,1,0:T(8,128)(2,1)} %broadcast_in_dim.15), calls=%async_computation.1 | async-start | bytes 524288 | tf_op jit(solution)/shard_map/all_to_all | solution.py:163
  177.5 9.8 %collective-permute-start.13 = (f32[64,256]{1,0:T(8,128)S(1)}, f32[64,256]{1,0:T(8,128)S(1)}, u32[]{:S(2)}, u32[]{:S(2)}) collective-permute-start(f32[64,256]{1,0:T(8,128)S(1)} %get-tuple-element.53), channel_id=1, source_target_pairs={{0,1},{1,0},{2,3},{3,2},{4,5},{5,4},{6,7},{7,6},{8,9},{9,8},{10,11... | collective-permute-start | bytes 196616 | tf_op jit(solution)/shard_map/ppermute | solution.py:241
  186.6 1.5 collective-permute-start.14
  188.1 1.1 copy-start.5
  189.3 1.1 copy-start.8
where the time goes:
time: 202 us; the launch traced here: 201 us
  waiting for transfers between devices  98 us (49%)
  starting transfers between devices  50.4 us (25%)
  Pallas kernels  25.8 us (13%)
  local copies, waits for them, and re-layouts  24 us (12%)
  other arithmetic  2.35 us (1%)
    ppermute x11, waiting for transfers between devices, sent(): return lax.ppermute(x, 'scan', [(i, i ^ k) for i in range(count)])  72 us
    all_to_all x1, starting transfers between devices, per_device(): pieces = lax.all_to_all(both, 'scan', 0, 0, tiled=True)  26.4 us
    ppermute x11, starting transfers between devices, sent(): return lax.ppermute(x, 'scan', [(i, i ^ k) for i in range(count)])  20.2 us
    squeeze x8, local copies, waits for them, and re-layouts, per_device(): block = lax.dynamic_index_in_dim(blocks, place, 0, keepdims=False)  15.7 us
    all_to_all x1, waiting for transfers between devices, per_device(): pieces = lax.all_to_all(both, 'scan', 0, 0, tiled=True)  14.8 us
    pallas_call x4, Pallas kernels, per_device(): pl.pallas_call(functools.partial(first_kernel, scale, pad, bool(sums)), o...  13.4 us
    pallas_call x1, Pallas kernels, per_device(): pl.pallas_call(functools.partial(second_kernel, scale, pad), out_shape=ja...  11 us
    all_to_all x1, waiting for transfers between devices, gathered(): return lax.all_to_all(copies, 'scan', 0, 0, tiled=True)  9.09 us
  transfers between devices with their start and end apart: 17, of which 8 were waited for; matrix products, arithmetic and copies ran while one was open for 8% of the time, Pallas kernels for 7%

commit v1 on v0

--- a/solution.py
+++ b/solution.py
@@ -12,10 +12,19 @@
 PAIR = 2 * LAG
 
 SWAP = [(0, 1), (1, 0)]
+LIMIT = 24 << 20
 
 VMEM = pl.BlockSpec(memory_space=pltpu.VMEM)
 SMEM = pl.BlockSpec(memory_space=pltpu.SMEM)
 ANY = pl.BlockSpec(memory_space=pl.ANY)
+
+
+def padded_rows(rows):
+    return -(-rows // PAIR) * PAIR
+
+
+def late_rows(rows):
+    return rows // 6 // 16 * 16
 
 
 def aligned(start):
@@ -68,7 +77,7 @@
     datas, (give, keep, total, resid) = rest[:-4], rest[-4:]
     lagrows = w.shape[1]
     _, comps, half = give.shape
-    _, width = datas[0].shape
+    width = datas[0].shape[1]
     count = lagrows // (2 * comps)
     lead = total.shape[1] - width - PAIR
     if chained:
@@ -81,10 +90,14 @@
     for i, data in enumerate(datas):
         source = ids[i]
         stack = lagged_tile(pairs, pad + source * width, width, count)
-        recon = jnp.dot(w[...], stack, preferred_element_type=jnp.float32)
-        resid[...] = (scale * recon - data[...].astype(jnp.float32)).astype(jnp.bfloat16)
+        rows = data.shape[0]
+        padded = padded_rows(rows)
+        recon = jnp.dot(w[:rows, :], stack, preferred_element_type=jnp.float32)
+        resid[:rows, :] = (scale * recon - data[...].astype(jnp.float32)).astype(jnp.bfloat16)
+        if padded > rows:
+            resid[rows:padded, :] = jnp.zeros((padded - rows, width), jnp.bfloat16)
         total[...] = jnp.zeros_like(total)
-        prods = jnp.dot(wt[...], resid[...], preferred_element_type=jnp.float32)
+        prods = jnp.dot(wt[:, :padded], resid[:padded, :], preferred_element_type=jnp.float32)
         for p in range(count):
             at = lead - p * PAIR
             total[:, at : at + width] += prods[p * 2 * comps : (p + 1) * 2 * comps]
@@ -109,32 +122,59 @@
                 fold((give, keep))
 
 
-def second_kernel(scale, pad, core, ids, w, rate, mine, other, *rest):
-    blocks, comps, half = mine.shape
+def step_two(scale, w, stack, data, total):
+    recon = jnp.dot(w, stack, preferred_element_type=jnp.float32)
+    resid = (scale * recon - data.astype(jnp.float32)).astype(jnp.bfloat16)
+    total[...] += lax.dot_general(
+        resid, stack, (((1,), (1,)), ((), ())), preferred_element_type=jnp.float32
+    )
+
+
+def fetch(sources, held, sems):
+    for i, source in enumerate(sources):
+        pltpu.make_async_copy(source, held.at[i], sems.at[i]).start()
+
+
+def late_kernel(scale, pad, early, core, ids, w, mine, other, *rest):
+    comps, half = mine.shape[1:]
     width = 2 * half
-    datas, (out, pairs, total, held, sems) = rest[:blocks], rest[blocks:]
-    _, lagrows = w.shape
+    spectra, (pairs, kept, given, total, held, sems) = rest[:-6], rest[-6:]
+    late, lagrows = kept.shape
     count = lagrows // (2 * comps)
-    copies = [pltpu.make_async_copy(d, held.at[i], sems.at[i]) for i, d in enumerate(datas)]
-    for copy in copies:
-        copy.start()
+    fetch([data.at[early : early + 2 * late, :] for data in spectra], held, sems)
     fill_stack(core[0], lambda e: e, mine, other, pairs, pad)
     total[...] = jnp.zeros_like(total)
 
     def one(i, _):
         pltpu.make_async_copy(held.at[i], held.at[i], sems.at[i]).wait()
         stack = lagged_tile(pairs, pad + ids[i] * width, width, count)
-        recon = jnp.dot(w[...], stack, preferred_element_type=jnp.float32)
-        resid = (scale * recon - held[i].astype(jnp.float32)).astype(jnp.bfloat16)
-        total[...] += lax.dot_general(
-            resid, stack, (((1,), (1,)), ((), ())), preferred_element_type=jnp.float32
-        )
+        step_two(scale, w[early : early + 2 * late, :], stack, held[i], total)
         return 0
 
-    lax.fori_loop(0, blocks, one, 0)
+    lax.fori_loop(0, len(spectra), one, 0)
+    kept[...] = total[:late, :]
+    given[...] = total[late:, :]
+
+
+def second_kernel(scale, pad, early, ids, w, rate, pairs, *rest):
+    spectra, (out, total, held, sems) = rest[:-4], rest[-4:]
+    lagrows = w.shape[1]
+    comps = rate.shape[1]
+    width = spectra[0].shape[1]
+    count = lagrows // (2 * comps)
+    fetch([data.at[:early, :] for data in spectra], held, sems)
+    total[...] = jnp.zeros_like(total)
+
+    def one(i, _):
+        pltpu.make_async_copy(held.at[i], held.at[i], sems.at[i]).wait()
+        stack = lagged_tile(pairs, pad + ids[i] * width, width, count)
+        step_two(scale, w[:early, :], stack, held[i], total)
+        return 0
+
+    lax.fori_loop(0, len(spectra), one, 0)
     rates = jnp.concatenate([rate[...]] * (lagrows // comps), 1)
-    out[...] = jnp.maximum(
-        w[...].astype(jnp.float32) - rates * (scale * total[...]), 0.0
+    out[:early, :] = jnp.maximum(
+        w[:early, :].astype(jnp.float32) - rates * (scale * total[...]), 0.0
     ).astype(jnp.bfloat16)
 
 
@@ -180,8 +220,10 @@
         return me ^ jnp.array(ks, jnp.int32)
 
     own = templates.reshape(rows, lagrows)
-    own_t = own.T
     act_half = lax.dynamic_slice(activations, (0, core * half), (comps, half))
+    across = count // 2
+    late = late_rows(rows)
+    early = rows - late
 
     rounded = act_half.astype(jnp.bfloat16)
     even = list(range(0, count, 2))
@@ -195,9 +237,18 @@
             landed[order[i - 1]] = sent(block, count, order[i - 1])
         if i == 1:
             column = jnp.stack([rounded] + [sent(rounded, count, e) for e in even[1:]])
-        block = lax.dynamic_index_in_dim(blocks, place, 0, keepdims=False)
+            theirs = sent(own[early:], count, across)
+        if k >= across:
+            block = lax.dynamic_slice(blocks, (place, 0, 0), (1, early, width))[0]
+        else:
+            block = lax.dynamic_index_in_dim(blocks, place, 0, keepdims=False)
+            extra = lax.dynamic_slice(blocks, (place ^ across, early, 0), (1, late, width))[0]
+            block = jnp.concatenate([block, extra], 0)
     landed[0] = block
     beside = sent(column, count, 1)
+    blank = jnp.zeros((padded_rows(rows + late) - rows - late, lagrows), jnp.bfloat16)
+    all_rows = jnp.concatenate([own, theirs, blank], 0)
+    all_rows_t = all_rows.T
 
     mine = jnp.concatenate([column, beside], 0)
     other = lax.ppermute(mine, "mz", SWAP)
@@ -217,19 +268,21 @@
     groups[0] = [0] + groups[0]
     sums = ()
     for ks in groups:
-        sums = pl.pallas_call(
+        call = pl.pallas_call(
             functools.partial(first_kernel, scale, pad, bool(sums)),
             out_shape=[jax.ShapeDtypeStruct(part, jnp.float32)] * 2,
             in_specs=[SMEM, SMEM] + [VMEM] * (3 + len(sums) + len(ks)),
             out_specs=[VMEM] * 2,
             scratch_shapes=[
                 pltpu.VMEM((2 * comps, lead + width + PAIR), jnp.float32),
-                pltpu.VMEM((rows, width), jnp.bfloat16),
+                pltpu.VMEM((all_rows.shape[0], width), jnp.bfloat16),
             ],
             cost_estimate=cost(rows, lagrows, width * len(ks)),
-            compiler_params=pltpu.CompilerParams(vmem_limit_bytes=24 << 20),
+            compiler_params=pltpu.CompilerParams(vmem_limit_bytes=LIMIT),
             name="first",
-        )(core_id, ids(ks), own, own_t, pairs, *sums, *[landed[k] for k in ks])
+        )
+        data = [landed[k] for k in ks]
+        sums = call(core_id, ids(ks), all_rows, all_rows_t, pairs, *sums, *data)
 
     give, keep = sums
     both = keep + lax.ppermute(give, "mz", SWAP)
@@ -245,28 +298,44 @@
         jnp.concatenate([new_other, new_half], 1),
     )
 
-    new_w = pl.pallas_call(
-        functools.partial(second_kernel, scale, pad),
+    near = [0] + [k for k in order if k < across]
+    sums_shape = jax.ShapeDtypeStruct((late, lagrows), jnp.float32)
+    pairs_new, kept, given = pl.pallas_call(
+        functools.partial(late_kernel, scale, pad, early),
+        out_shape=[jax.ShapeDtypeStruct(stack_shape, jnp.bfloat16), sums_shape, sums_shape],
+        in_specs=[SMEM, SMEM] + [VMEM] * 3 + [ANY] * len(near),
+        out_specs=[VMEM] * 3,
+        scratch_shapes=[
+            pltpu.VMEM((2 * late, lagrows), jnp.float32),
+            pltpu.VMEM((len(near), 2 * late, width), jnp.bfloat16),
+            pltpu.SemaphoreType.DMA((len(near),)),
+        ],
+        cost_estimate=cost(2 * late, lagrows, width * len(near)),
+        compiler_params=pltpu.CompilerParams(vmem_limit_bytes=LIMIT),
+        name="late",
+    )(core_id, ids(near), all_rows, mine_new, other_new, *[landed[k] for k in near])
+    taken = sent(given, count, across)
+
+    use = [0] + order
+    second = pl.pallas_call(
+        functools.partial(second_kernel, scale, pad, early),
         out_shape=jax.ShapeDtypeStruct((rows, lagrows), jnp.bfloat16),
-        in_specs=[SMEM, SMEM] + [VMEM] * 4 + [ANY] * count,
+        in_specs=[SMEM] + [VMEM] * 3 + [ANY] * count,
         out_specs=VMEM,
         scratch_shapes=[
-            pltpu.VMEM(stack_shape, jnp.bfloat16),
-            pltpu.VMEM((rows, lagrows), jnp.float32),
-            pltpu.VMEM((count, rows, width), jnp.bfloat16),
+            pltpu.VMEM((early, lagrows), jnp.float32),
+            pltpu.VMEM((count, early, width), jnp.bfloat16),
             pltpu.SemaphoreType.DMA((count,)),
         ],
-        cost_estimate=cost(rows, lagrows, width * count),
-        compiler_params=pltpu.CompilerParams(vmem_limit_bytes=32 << 20),
+        cost_estimate=cost(early, lagrows, width * count),
+        compiler_params=pltpu.CompilerParams(vmem_limit_bytes=LIMIT),
         name="second",
-    )(
-        core_id,
-        ids([0] + order),
-        own,
-        w_rate[None, :],
-        mine_new,
-        other_new,
-        *[landed[k] for k in [0] + order],
+    )
+    new_w = second(ids(use), all_rows, w_rate[None, :], pairs_new, *[landed[k] for k in use])
+    rates = jnp.tile(w_rate, lags)[None, :]
+    new_late = own[early:].astype(jnp.float32) - rates * (scale * (kept + taken))
+    new_w = lax.dynamic_update_slice(
+        new_w, jnp.maximum(new_late, 0.0).astype(jnp.bfloat16), (early, 0)
     )
     return (new_h, new_w.reshape(templates.shape))
 

time: 202 us -> 197 us (0.975)
  waiting for transfers between devices: 98 us -> 83 us
  other arithmetic: 2.35 us -> 8.67 us
  local copies, waits for them, and re-layouts: 24 us -> 27.8 us
  starting transfers between devices: 50.4 us -> 47.2 us
  Pallas kernels: 25.8 us -> 28.6 us
    ppermute x11 -> x13, waiting for transfers between devices: 72 us -> 56.6 us  [sent(): return lax.ppermute(x, 'scan', [(i, i ^ k) for i in range(count)])]
    squeeze x0 -> x8, local copies, waits for them, and re-layouts: none -> 11.8 us  [the longest x4 8.11 us: per_device(): block = lax.dynamic_slice(blocks, (place, 0, 0), (1, early, width))[0]]
    squeeze x8 -> x4, local copies, waits for them, and re-layouts: 15.7 us -> 4.74 us  [per_device(): block = lax.dynamic_index_in_dim(blocks, place, 0, keepdims=False)]
    all_to_all x1, starting transfers between devices: 26.4 us -> 17.3 us  [per_device(): pieces = lax.all_to_all(both, 'scan', 0, 0, tiled=True)]
    ppermute x11 -> x13, starting transfers between devices: 20.2 us -> 26 us  [sent(): return lax.ppermute(x, 'scan', [(i, i ^ k) for i in range(count)])]
    concatenate x0 -> x4, other arithmetic: none -> 3.09 us  [per_device(): block = jnp.concatenate([block, extra], 0)]
    pallas_call x5 -> x6, Pallas kernels: 24.4 us -> 27.2 us  [the longest x4 14 us: per_device(): sums = call(core_id, ids(ks), all_rows, all_rows_t, pairs, *sums, *data)]
    transpose x0 -> x1, other arithmetic: none -> 2.23 us  [per_device(): all_rows_t = all_rows.T]
  transfers between devices with their start and end apart: 17 -> 19, of which waited for: 8 -> 11; matrix products, arithmetic and copies ran while one was open for 8% -> 12% of each run, Pallas kernels for 7% -> 12%
where the time goes in v1:
time: 197 us; the launch traced here: 196 us
  waiting for transfers between devices  83 us (42%)
  starting transfers between devices  47.2 us (24%)
  Pallas kernels  28.6 us (15%)
  local copies, waits for them, and re-layouts  27.8 us (14%)
  other arithmetic  8.67 us (4%)
    ppermute x13, waiting for transfers between devices, sent(): return lax.ppermute(x, 'scan', [(i, i ^ k) for i in range(count)])  56.6 us
    ppermute x13, starting transfers between devices, sent(): return lax.ppermute(x, 'scan', [(i, i ^ k) for i in range(count)])  26 us
    all_to_all x1, starting transfers between devices, per_device(): pieces = lax.all_to_all(both, 'scan', 0, 0, tiled=True)  17.3 us
    all_to_all x1, waiting for transfers between devices, per_device(): pieces = lax.all_to_all(both, 'scan', 0, 0, tiled=True)  14.8 us
    pallas_call x4, Pallas kernels, per_device(): sums = call(core_id, ids(ks), all_rows, all_rows_t, pairs, *sums, *data)  14 us
    pallas_call x1, Pallas kernels, per_device(): second(ids(use), all_rows, w_rate[None, :], pairs_new, *[landed[k] for k...  9.62 us
    all_to_all x1, waiting for transfers between devices, gathered(): return lax.all_to_all(copies, 'scan', 0, 0, tiled=True)  8.98 us
    squeeze x4, local copies, waits for them, and re-layouts, per_device(): block = lax.dynamic_slice(blocks, (place, 0, 0), (1, early, width))[0]  8.11 us
  transfers between devices with their start and end apart: 19, of which 11 were waited for; matrix products, arithmetic and copies ran while one was open for 12% of the time, Pallas kernels for 12%

profile of v1, /device:TPU:0, one launch (start us, length us, event | category | flops | bytes accessed | tf_op | source)
XLA Modules:
  0.0 196.3 jit_solution(11123341750240895245)
XLA Ops:
  0.6 0.9 dynamic-slice_convert_fusion
  1.5 2.0 %dynamic-slice_bitcast_fusion.7 = bf16[640,512]{1,0:T(8,128)(2,1)} fusion(bf16[8,768,512]{2,1,0:T(8,128)(2,1)} %bitcast.49, s32[]{:T(128)S(6)} %select_n.50), kind=kLoop, calls=%fused_computation.12 | loop fusion | bytes 1310724 | tf_op jit(solution)/shard_map/squeeze | solution.py:242
  3.5 3.1 %collective-permute-start.1 = (bf16[64,256]{1,0:T(8,128)(2,1)S(1)}, bf16[64,256]{1,0:T(8,128)(2,1)S(1)}, u32[]{:S(2)}, u32[]{:S(2)}) collective-permute-start(bf16[64,256]{1,0:T(8,128)(2,1)S(1)} %dynamic-slice_convert_fusion), channel_id=1, source_target_pairs={{0,4},{2,6},{4,0},{6,2},{8,12},{10,14},{12,8},{14,10},{1,5},{3,7},... | collective-permute-start | bytes 98312 | tf_op jit(solution)/shard_map/ppermute | solution.py:198
  6.5 2.6 %collective-permute-start.2 = (bf16[64,256]{1,0:T(8,128)(2,1)S(1)}, bf16[64,256]{1,0:T(8,128)(2,1)S(1)}, u32[]{:S(2)}, u32[]{:S(2)}) collective-permute-start(bf16[64,256]{1,0:T(8,128)(2,1)S(1)} %dynamic-slice_convert_fusion), channel_id=1, source_target_pairs={{0,8},{2,10},{4,12},{6,14},{8,0},{10,2},{12,4},{14,6},{1,9},{3,11}... | collective-permute-start | bytes 98312 | tf_op jit(solution)/shard_map/ppermute | solution.py:198
  9.1 1.2 dynamic-slice_bitcast_fusion.3
  10.3 0.9 dynamic-slice_bitcast_fusion.11
  11.2 1.0 pad_maximum_fusion.1
  12.2 0.9 collective-permute-start.7
  13.1 3.5 %collective-permute-start.6 = (bf16[640,512]{1,0:T(8,128)(2,1)}, bf16[640,512]{1,0:T(8,128)(2,1)S(1)}, u32[]{:S(2)}, u32[]{:S(2)}) collective-permute-start(bf16[640,512]{1,0:T(8,128)(2,1)} %dynamic-slice_bitcast_fusion.7), channel_id=1, source_target_pairs={{0,8},{2,10},{4,12},{6,14},{8,0},{10,2},{12,4},{14,6},{1,9},{3,11}... | collective-permute-start | bytes 1966088 | tf_op jit(solution)/shard_map/ppermute | solution.py:198
  16.6 2.0 %dynamic-slice_bitcast_fusion.6 = bf16[640,512]{1,0:T(8,128)(2,1)} fusion(bf16[8,768,512]{2,1,0:T(8,128)(2,1)} %bitcast.52, s32[]{:T(128)S(6)} %select_n.53), kind=kLoop, calls=%fused_computation.11 | loop fusion | bytes 1310724 | tf_op jit(solution)/shard_map/squeeze | solution.py:242
  18.6 1.2 dynamic-slice_bitcast_fusion.2
  19.8 0.9 dynamic-slice_bitcast_fusion.10
  20.7 1.0 pad_maximum_fusion.2
  21.7 2.1 %dynamic-slice_bitcast_fusion.5 = bf16[640,512]{1,0:T(8,128)(2,1)} fusion(bf16[8,768,512]{2,1,0:T(8,128)(2,1)} %bitcast.55, s32[]{:T(128)S(6)} %select_n.56), kind=kLoop, calls=%fused_computation.10 | loop fusion | bytes 1310724 | tf_op jit(solution)/shard_map/squeeze | solution.py:242
  23.8 1.2 dynamic-slice_bitcast_fusion.1
  25.0 0.9 dynamic-slice_bitcast_fusion.9
  26.0 0.9 slice_bitcast_fusion
  26.9 1.0 pad_maximum_fusion.3
  28.0 1.7 collective-permute-start.9
  29.7 0.4 collective-permute-start.4
  30.1 4.7 %collective-permute-done.4 = bf16[4,64,256]{2,1,0:T(8,128)(2,1)S(1)} collective-permute-done((bf16[4,64,256]{2,1,0:T(8,128)(2,1)S(1)}, bf16[4,64,256]{2,1,0:T(8,128)(2,1)S(1)}, u32[]{:S(2)}, u32[]{:S(2)}) %collective-permute-start.4) | collective-permute-done | bytes 131104 | tf_op jit(solution)/shard_map/ppermute | solution.py:198
  34.8 0.1 collective-permute-start.5
  34.9 2.1 %dynamic-slice_bitcast_fusion.4 = bf16[640,512]{1,0:T(8,128)(2,1)} fusion(bf16[8,768,512]{2,1,0:T(8,128)(2,1)} %bitcast.58, s32[]{:T(128)S(6)} %select_n.59), kind=kLoop, calls=%fused_computation.9 | loop fusion | bytes 1310724 | tf_op jit(solution)/shard_map/squeeze | solution.py:242
  36.9 14.0 %collective-permute-done = bf16[128,512]{1,0:T(8,128)(2,1)S(1)} collective-permute-done((bf16[128,512]{1,0:T(8,128)(2,1)S(1)}, bf16[128,512]{1,0:T(8,128)(2,1)S(1)}, u32[]{:S(2)}, u32[]{:S(2)}) %collective-permute-start) | collective-permute-done | bytes 131104 | tf_op jit(solution)/shard_map/ppermute | solution.py:198
  50.9 4.3 %collective-permute-start.8 = (bf16[640,512]{1,0:T(8,128)(2,1)}, bf16[640,512]{1,0:T(8,128)(2,1)}, u32[]{:S(2)}, u32[]{:S(2)}) collective-permute-start(bf16[640,512]{1,0:T(8,128)(2,1)} %dynamic-slice_bitcast_fusion.6), channel_id=1, source_target_pairs={{0,10},{2,8},{4,14},{6,12},{8,2},{10,0},{12,6},{14,4},{1,11},{3,9}... | collective-permute-start | bytes 1966088 | tf_op jit(solution)/shard_map/ppermute | solution.py:198
  55.3 0.5 collective-permute-start.11
  55.8 0.9 dynamic-slice_bitcast_fusion.8
  56.7 1.2 dynamic-slice_bitcast_fusion
  57.9 0.8 copy-done.7
  58.7 2.9 %collective-permute-start.10 = (bf16[640,512]{1,0:T(8,128)(2,1)}, bf16[640,512]{1,0:T(8,128)(2,1)}, u32[]{:S(2)}, u32[]{:S(2)}) collective-permute-start(bf16[640,512]{1,0:T(8,128)(2,1)} %dynamic-slice_bitcast_fusion.5), channel_id=1, source_target_pairs={{0,12},{2,14},{4,8},{6,10},{8,4},{10,6},{12,0},{14,2},{1,13},{3,15... | collective-permute-start | bytes 1966088 | tf_op jit(solution)/shard_map/ppermute | solution.py:198
  61.8 0.9 copy-done
  62.7 5.0 %collective-permute-start.12 = (bf16[640,512]{1,0:T(8,128)(2,1)}, bf16[640,512]{1,0:T(8,128)(2,1)S(1)}, u32[]{:S(2)}, u32[]{:S(2)}) collective-permute-start(bf16[640,512]{1,0:T(8,128)(2,1)} %dynamic-slice_bitcast_fusion.4), channel_id=1, source_target_pairs={{0,14},{2,12},{4,10},{6,8},{8,6},{10,4},{12,2},{14,0},{1,15},{3,13... | collective-permute-start | bytes 1966088 | tf_op jit(solution)/shard_map/ppermute | solution.py:198
  67.7 2.2 %fusion.2 = (bf16[512,896]{0,1:T(8,128)(2,1)}, bf16[896,512]{1,0:T(8,128)(2,1)S(1)}) fusion(bf16[128,512]{1,0:T(8,128)(2,1)S(1)} %collective-permute-done, bf16[768,512]{1,0:T(8,128)(2,1)} %bitcast.61), kind=kLoop, calls=%fused_computation.38 | loop fusion | flops 1835008 | bytes 2752512 | tf_op jit(solution)/shard_map/transpose | solution.py:251
  70.0 1.5 copy.17.wt
  71.5 0.9 copy-done.4
  72.4 0.9 copy-done.6
  73.4 1.4 stack.21.pairs
  74.8 1.2 copy-done.1
  76.0 1.1 copy-done.8
  77.1 4.5 %first.4 = (f32[8,64,256]{2,1,0:T(8,128)S(1)}, f32[8,64,256]{2,1,0:T(8,128)S(1)}) custom-call(s32[1]{0:T(128)} %bitcast.core, s32[3]{0:T(128)S(1)} %broadcast_xor_fusion.1.ids, bf16[896,512]{1,0:T(8,128)(2,1)S(1)} %get-tuple-element.61.w, bf16[512,896]{1,0:T(8,128)(2,1)S(1)} %copy.17.wt, bf16[128,4608]{1,0:T(8,128)(2,1)S(1)} %stack.21.pairs, ...), custom_call_target="tpu_custom_call" | custom-call | flops 2415919104 | bytes 2359296 | tf_op jit(solution)/shard_map/first/pallas_call | solution.py:285
  81.6 4.0 %collective-permute-done.8.rest_2_.rest_3_ = bf16[640,512]{1,0:T(8,128)(2,1)} collective-permute-done((bf16[640,512]{1,0:T(8,128)(2,1)}, bf16[640,512]{1,0:T(8,128)(2,1)}, u32[]{:S(2)}, u32[]{:S(2)}) %collective-permute-start.8) | collective-permute-done | bytes 655392 | tf_op jit(solution)/shard_map/ppermute | solution.py:198
  85.6 0.4 collective-permute-done.9.rest_3_.rest_2_.rest_4_
  86.0 4.1 %first.5 = (f32[8,64,256]{2,1,0:T(8,128)S(1)}, f32[8,64,256]{2,1,0:T(8,128)S(1)}) custom-call(s32[1]{0:T(128)} %bitcast.core, s32[2]{0:T(128)S(1)} %broadcast_xor_fusion.2.ids, bf16[896,512]{1,0:T(8,128)(2,1)S(1)} %get-tuple-element.61.w, bf16[512,896]{1,0:T(8,128)(2,1)S(1)} %copy.17.wt, bf16[128,4608]{1,0:T(8,128)(2,1)S(1)} %stack.21.pairs, ...), custom_call_target="tpu_custom_call" | custom-call | flops 1610612736 | bytes 1572864 | tf_op jit(solution)/shard_map/first/pallas_call | solution.py:285
  90.1 12.3 %collective-permute-done.10.rest_2_.rest_5_ = bf16[640,512]{1,0:T(8,128)(2,1)} collective-permute-done((bf16[640,512]{1,0:T(8,128)(2,1)}, bf16[640,512]{1,0:T(8,128)(2,1)}, u32[]{:S(2)}, u32[]{:S(2)}) %collective-permute-start.10) | collective-permute-done | bytes 655392 | tf_op jit(solution)/shard_map/ppermute | solution.py:198
  102.4 17.0 %collective-permute-done.11.rest_3_.rest_6_ = bf16[896,512]{1,0:T(8,128)(2,1)} collective-permute-done((bf16[896,512]{1,0:T(8,128)(2,1)}, bf16[896,512]{1,0:T(8,128)(2,1)}, u32[]{:S(2)}, u32[]{:S(2)}) %collective-permute-start.11) | collective-permute-done | bytes 917536 | tf_op jit(solution)/shard_map/ppermute | solution.py:198
  119.4 4.1 %first.6 = (f32[8,64,256]{2,1,0:T(8,128)S(1)}, f32[8,64,256]{2,1,0:T(8,128)S(1)}) custom-call(s32[1]{0:T(128)} %bitcast.core, s32[2]{0:T(128)S(1)} %broadcast_xor_fusion.3.ids, bf16[896,512]{1,0:T(8,128)(2,1)S(1)} %get-tuple-element.61.w, bf16[512,896]{1,0:T(8,128)(2,1)S(1)} %copy.17.wt, bf16[128,4608]{1,0:T(8,128)(2,1)S(1)} %stack.21.pairs, ...), custom_call_target="tpu_custom_call" | custom-call | flops 1610612736 | bytes 1572864 | tf_op jit(solution)/shard_map/first/pallas_call | solution.py:285
  123.5 1.3 first.7
  124.9 1.9 collective-permute-done.13
  126.8 0.9 add.59
  127.7 17.3 %all-to-all-start = ((f32[8,64,256]{2,1,0:T(8,128)}), f32[8,64,256]{2,1,0:T(8,128)S(1)}, u32[]{:S(2)}, u32[]{:S(2)}) async-start(f32[8,64,256]{2,1,0:T(8,128)} %add.59), calls=%async_computation | async-start | bytes 1048576 | tf_op jit(solution)/shard_map/all_to_all | solution.py:289
  145.1 14.8 %all-to-all-done = f32[8,64,256]{2,1,0:T(8,128)S(1)} async-done(((f32[8,64,256]{2,1,0:T(8,128)}), f32[8,64,256]{2,1,0:T(8,128)S(1)}, u32[]{:S(2)}, u32[]{:S(2)}) %all-to-all-start) | async-done | bytes 524320 | tf_op jit(solution)/shard_map/all_to_all | solution.py:289
  159.9 0.1 fusion.3
  160.0 0.7 broadcast_in_dim.15
  160.7 3.6 %all-to-all-start.1 = ((bf16[8,64,256]{2,1,0:T(8,128)(2,1)}), bf16[8,64,256]{2,1,0:T(8,128)(2,1)S(1)}, u32[]{:S(2)}, u32[]{:S(2)}) async-start(bf16[8,64,256]{2,1,0:T(8,128)(2,1)} %broadcast_in_dim.15), calls=%async_computation.1 | async-start | bytes 524288 | tf_op jit(solution)/shard_map/all_to_all | solution.py:203
  164.4 9.0 %all-to-all-done.1.mine = bf16[8,64,256]{2,1,0:T(8,128)(2,1)S(1)} async-done(((bf16[8,64,256]{2,1,0:T(8,128)(2,1)}), bf16[8,64,256]{2,1,0:T(8,128)(2,1)S(1)}, u32[]{:S(2)}, u32[]{:S(2)}) %all-to-all-start.1) | async-done | bytes 262176 | tf_op jit(solution)/shard_map/all_to_all | solution.py:203
  173.5 0.1 mul.37
  173.5 0.7 maximum_select_fusion
  174.2 0.8 collective-permute-done.15.other
  175.0 1.2 copy-done.2
  176.1 3.6 %late.1 = (bf16[128,4608]{1,0:T(8,128)(2,1)S(1)}, f32[128,512]{1,0:T(8,128)S(1)}, f32[128,512]{1,0:T(8,128)S(1)}) custom-call(s32[1]{0:T(128)} %bitcast.core, s32[4]{0:T(128)S(1)} %broadcast_xor_fusion.ids, bf16[896,512]{1,0:T(8,128)(2,1)S(1)} %get-tuple-element.61.w, bf16[8,64,256]{2,1,0:T(8,128)(2,1)S(1)} %all-to-all-done.1.mine, ...), custom_call_target="tpu_custom_call" | custom-call | flops 1073741824 | bytes 1048576 | tf_op jit(solution)/shard_map/late/pallas_call | solution.py:303
  179.8 1.1 collective-permute-start.16
  180.9 9.6 %second.1 = bf16[768,512]{1,0:T(8,128)(2,1)} custom-call(s32[8]{0:T(128)S(1)} %broadcast_xor_fusion.4.ids, bf16[896,512]{1,0:T(8,128)(2,1)S(1)} %get-tuple-element.61.w, f32[1,64]{1,0:T(1,128)S(1)} %bitcast.48, bf16[128,4608]{1,0:T(8,128)(2,1)S(1)} %get-tuple-element.55.pairs, bf16[896,512]{1,0:T(8,128)(2,1)S(1)} %pad_maximum_fusion.4.rest_0_, ...), custom_call_target="tpu_custom_call" | custom-call | flops 5368709120 | bytes 5242880 | tf_op jit(solution)/shard_map/second/pallas_call | solution.py:334
  190.5 4.2 %collective-permute-done.16 = f32[128,512]{1,0:T(8,128)S(1)} collective-permute-done((f32[128,512]{1,0:T(8,128)S(1)}, f32[128,512]{1,0:T(8,128)S(1)}, u32[]{:S(2)}, u32[]{:S(2)}) %collective-permute-start.16) | collective-permute-done | bytes 262176 | tf_op jit(solution)/shard_map/ppermute | solution.py:198
  194.7 1.6 fusion.1
  (61 shorter events, 0.4 us)
Async XLA Ops:
  3.5 24.5 %collective-permute-start.1 = (bf16[64,256]{1,0:T(8,128)(2,1)S(1)}, bf16[64,256]{1,0:T(8,128)(2,1)S(1)}, u32[]{:S(2)}, u32[]{:S(2)}) collective-permute-start(bf16[64,256]{1,0:T(8,128)(2,1)S(1)} %dynamic-slice_convert_fusion), channel_id=1, source_target_pairs={{0,4},{2,6},{4,0},{6,2},{8,12},{10,14},{12,8},{14,10},{1,5},{3,7},... | collective-permute-start | bytes 98312 | tf_op jit(solution)/shard_map/ppermute | solution.py:198
  6.5 21.4 %collective-permute-start.2 = (bf16[64,256]{1,0:T(8,128)(2,1)S(1)}, bf16[64,256]{1,0:T(8,128)(2,1)S(1)}, u32[]{:S(2)}, u32[]{:S(2)}) collective-permute-start(bf16[64,256]{1,0:T(8,128)(2,1)S(1)} %dynamic-slice_convert_fusion), channel_id=1, source_target_pairs={{0,8},{2,10},{4,12},{6,14},{8,0},{10,2},{12,4},{14,6},{1,9},{3,11}... | collective-permute-start | bytes 98312 | tf_op jit(solution)/shard_map/ppermute | solution.py:198
  9.1 20.6 %collective-permute-start.3 = (bf16[64,256]{1,0:T(8,128)(2,1)S(1)}, bf16[64,256]{1,0:T(8,128)(2,1)S(1)}, u32[]{:S(2)}, u32[]{:S(2)}) collective-permute-start(bf16[64,256]{1,0:T(8,128)(2,1)S(1)} %dynamic-slice_convert_fusion), channel_id=1, source_target_pairs={{0,12},{2,14},{4,8},{6,10},{8,4},{10,6},{12,0},{14,2},{1,13},{3,15... | collective-permute-start | bytes 98312 | tf_op jit(solution)/shard_map/ppermute | solution.py:198
  12.2 49.5 %collective-permute-start.7 = (bf16[896,512]{1,0:T(8,128)(2,1)}, bf16[896,512]{1,0:T(8,128)(2,1)S(1)}, u32[]{:S(2)}, u32[]{:S(2)}) collective-permute-start(bf16[896,512]{1,0:T(8,128)(2,1)} %pad_maximum_fusion.1), channel_id=1, source_target_pairs={{0,4},{2,6},{4,0},{6,2},{8,12},{10,14},{12,8},{14,10},{1,5},{3,7},... | collective-permute-start | bytes 2752520 | tf_op jit(solution)/shard_map/ppermute | solution.py:198
  13.1 44.8 %collective-permute-start.6 = (bf16[640,512]{1,0:T(8,128)(2,1)}, bf16[640,512]{1,0:T(8,128)(2,1)S(1)}, u32[]{:S(2)}, u32[]{:S(2)}) collective-permute-start(bf16[640,512]{1,0:T(8,128)(2,1)} %dynamic-slice_bitcast_fusion.7), channel_id=1, source_target_pairs={{0,8},{2,10},{4,12},{6,14},{8,0},{10,2},{12,4},{14,6},{1,9},{3,11}... | collective-permute-start | bytes 1966088 | tf_op jit(solution)/shard_map/ppermute | solution.py:198
  21.7 4.2 %copy-start.18 = (s32[8]{0:T(128)S(1)}, s32[8]{0:T(128)}, u32[]{:S(2)}) copy-start(s32[8]{0:T(128)} %constant.64.clone) | copy-start | bytes 100
  21.7 4.2 %copy-start.17 = (s32[3]{0:T(128)S(1)}, s32[3]{0:T(128)}, u32[]{:S(2)}) copy-start(s32[3]{0:T(128)} %constant.65.clone) | copy-start | bytes 40
  21.7 5.2 %copy-start.16 = (s32[2]{0:T(128)S(1)}, s32[2]{0:T(128)}, u32[]{:S(2)}) copy-start(s32[2]{0:T(128)} %constant.66.clone) | copy-start | bytes 28
  26.9 10.0 %copy-start.15 = (s32[2]{0:T(128)S(1)}, s32[2]{0:T(128)}, u32[]{:S(2)}) copy-start(s32[2]{0:T(128)} %constant.67.clone) | copy-start | bytes 28
  27.9 23.0 %collective-permute-start = (bf16[128,512]{1,0:T(8,128)(2,1)S(1)}, bf16[128,512]{1,0:T(8,128)(2,1)S(1)}, u32[]{:S(2)}, u32[]{:S(2)}) collective-permute-start(bf16[128,512]{1,0:T(8,128)(2,1)S(1)} %slice_bitcast_fusion), channel_id=1, source_target_pairs={{0,8},{2,10},{4,12},{6,14},{8,0},{10,2},{12,4},{14,6},{1,9},{3,11}... | collective-permute-start | bytes 393224 | tf_op jit(solution)/shard_map/ppermute | solution.py:198
  28.0 58.0 %collective-permute-start.9 = (bf16[896,512]{1,0:T(8,128)(2,1)}, bf16[896,512]{1,0:T(8,128)(2,1)}, u32[]{:S(2)}, u32[]{:S(2)}) collective-permute-start(bf16[896,512]{1,0:T(8,128)(2,1)} %pad_maximum_fusion.2), channel_id=1, source_target_pairs={{0,6},{2,4},{4,2},{6,0},{8,14},{10,12},{12,10},{14,8},{1,7},{3,5},... | collective-permute-start | bytes 2752520 | tf_op jit(solution)/shard_map/ppermute | solution.py:198
  29.7 5.0 %collective-permute-start.4 = (bf16[4,64,256]{2,1,0:T(8,128)(2,1)S(1)}, bf16[4,64,256]{2,1,0:T(8,128)(2,1)S(1)}, u32[]{:S(2)}, u32[]{:S(2)}) collective-permute-start(bf16[4,64,256]{2,1,0:T(8,128)(2,1)S(1)} %pad_maximum_fusion.5), channel_id=1, source_target_pairs={{0,2},{2,0},{4,6},{6,4},{8,10},{10,8},{12,14},{14,12},{1,3},{3,1},... | collective-permute-start | bytes 393224 | tf_op jit(solution)/shard_map/ppermute | solution.py:198
  34.8 27.0 %copy-start.3 = (bf16[8,64,256]{2,1,0:T(8,128)(2,1)}, bf16[8,64,256]{2,1,0:T(8,128)(2,1)S(1)}, u32[]{:S(2)}) copy-start(bf16[8,64,256]{2,1,0:T(8,128)(2,1)S(1)} %constant_dynamic-update-slice_fusion.mine) | copy-start | bytes 786436
  34.8 20.5 %collective-permute-start.5 = (bf16[8,64,256]{2,1,0:T(8,128)(2,1)S(1)}, bf16[8,64,256]{2,1,0:T(8,128)(2,1)S(1)}, u32[]{:S(2)}, u32[]{:S(2)}) collective-permute-start(bf16[8,64,256]{2,1,0:T(8,128)(2,1)S(1)} %constant_dynamic-update-slice_fusion.mine), channel_id=1, source_target_pairs={{0,1},{1,0},{2,3},{3,2},{4,5},{5,4},{6,7},{7,6},{8,9},{9,8},{10,11... | collective-permute-start | bytes 786440 | tf_op jit(solution)/shard_map/ppermute | solution.py:254
  50.9 34.6 %collective-permute-start.8 = (bf16[640,512]{1,0:T(8,128)(2,1)}, bf16[640,512]{1,0:T(8,128)(2,1)}, u32[]{:S(2)}, u32[]{:S(2)}) collective-permute-start(bf16[640,512]{1,0:T(8,128)(2,1)} %dynamic-slice_bitcast_fusion.6), channel_id=1, source_target_pairs={{0,10},{2,8},{4,14},{6,12},{8,2},{10,0},{12,6},{14,4},{1,11},{3,9}... | collective-permute-start | bytes 1966088 | tf_op jit(solution)/shard_map/ppermute | solution.py:198
  55.3 6.5 %copy-start.5 = (bf16[8,64,256]{2,1,0:T(8,128)(2,1)}, bf16[8,64,256]{2,1,0:T(8,128)(2,1)S(1)}, u32[]{:S(2)}) copy-start(bf16[8,64,256]{2,1,0:T(8,128)(2,1)S(1)} %collective-permute-done.5.other) | copy-start | bytes 786436
  55.3 64.1 %collective-permute-start.11 = (bf16[896,512]{1,0:T(8,128)(2,1)}, bf16[896,512]{1,0:T(8,128)(2,1)}, u32[]{:S(2)}, u32[]{:S(2)}) collective-permute-start(bf16[896,512]{1,0:T(8,128)(2,1)} %pad_maximum_fusion.3), channel_id=1, source_target_pairs={{0,2},{2,0},{4,6},{6,4},{8,10},{10,8},{12,14},{14,12},{1,3},{3,1},... | collective-permute-start | bytes 2752520 | tf_op jit(solution)/shard_map/ppermute | solution.py:198
  57.9 0.8 copy-start.7
  58.7 43.7 %collective-permute-start.10 = (bf16[640,512]{1,0:T(8,128)(2,1)}, bf16[640,512]{1,0:T(8,128)(2,1)}, u32[]{:S(2)}, u32[]{:S(2)}) collective-permute-start(bf16[640,512]{1,0:T(8,128)(2,1)} %dynamic-slice_bitcast_fusion.5), channel_id=1, source_target_pairs={{0,12},{2,14},{4,8},{6,10},{8,4},{10,6},{12,0},{14,2},{1,13},{3,15... | collective-permute-start | bytes 1966088 | tf_op jit(solution)/shard_map/ppermute | solution.py:198
  61.8 0.9 copy-start
  62.7 60.8 %collective-permute-start.12 = (bf16[640,512]{1,0:T(8,128)(2,1)}, bf16[640,512]{1,0:T(8,128)(2,1)S(1)}, u32[]{:S(2)}, u32[]{:S(2)}) collective-permute-start(bf16[640,512]{1,0:T(8,128)(2,1)} %dynamic-slice_bitcast_fusion.4), channel_id=1, source_target_pairs={{0,14},{2,12},{4,10},{6,8},{8,6},{10,4},{12,2},{14,0},{1,15},{3,13... | collective-permute-start | bytes 1966088 | tf_op jit(solution)/shard_map/ppermute | solution.py:198
  71.5 1.0 copy-start.4
  72.4 0.9 copy-start.6
  74.8 1.2 copy-start.1
  76.0 1.1 copy-start.8
  124.8 20.2 %copy-start.12 = (f32[64]{0:T(128)S(1)}, f32[64]{0:T(128)}, u32[]{:S(2)}) copy-start(f32[64]{0:T(128)} %param.15) | copy-start | bytes 772
  124.9 35.0 %copy-start.11 = (f32[64,512]{1,0:T(8,128)S(1)}, f32[64,512]{1,0:T(8,128)}, u32[]{:S(2)}) copy-start(f32[64,512]{1,0:T(8,128)} %param.14) | copy-start | bytes 393220
  124.9 2.0 %collective-permute-start.13 = (f32[8,64,256]{2,1,0:T(8,128)S(1)}, f32[8,64,256]{2,1,0:T(8,128)S(1)}, u32[]{:S(2)}, u32[]{:S(2)}) collective-permute-start(f32[8,64,256]{2,1,0:T(8,128)S(1)} %get-tuple-element.54), channel_id=1, source_target_pairs={{0,1},{1,0},{2,3},{3,2},{4,5},{5,4},{6,7},{7,6},{8,9},{9,8},{10,11... | collective-permute-start | bytes 1572872 | tf_op jit(solution)/shard_map/ppermute | solution.py:288
  126.8 37.5 %copy-start.14 = (s32[4]{0:T(128)S(1)}, s32[4]{0:T(128)}, u32[]{:S(2)}) copy-start(s32[4]{0:T(128)} %constant.69.clone) | copy-start | bytes 52
  126.8 37.5 %copy-start.13 = (s32[8]{0:T(128)S(1)}, s32[8]{0:T(128)}, u32[]{:S(2)}) copy-start(s32[8]{0:T(128)} %constant.70.clone) | copy-start | bytes 100
  126.8 46.6 %copy-start.10 = (f32[64]{0:T(128)S(1)}, f32[64]{0:T(128)}, u32[]{:S(2)}) copy-start(f32[64]{0:T(128)} %param.16) | copy-start | bytes 772
  127.7 32.1 %all-to-all-start = ((f32[8,64,256]{2,1,0:T(8,128)}), f32[8,64,256]{2,1,0:T(8,128)S(1)}, u32[]{:S(2)}, u32[]{:S(2)}) async-start(f32[8,64,256]{2,1,0:T(8,128)} %add.59), calls=%async_computation | async-start | bytes 1048576 | tf_op jit(solution)/shard_map/all_to_all | solution.py:289
  160.7 12.7 %all-to-all-start.1 = ((bf16[8,64,256]{2,1,0:T(8,128)(2,1)}), bf16[8,64,256]{2,1,0:T(8,128)(2,1)S(1)}, u32[]{:S(2)}, u32[]{:S(2)}) async-start(bf16[8,64,256]{2,1,0:T(8,128)(2,1)} %broadcast_in_dim.15), calls=%async_computation.1 | async-start | bytes 524288 | tf_op jit(solution)/shard_map/all_to_all | solution.py:203
  164.4 9.2 %collective-permute-start.14 = (f32[64,256]{1,0:T(8,128)S(1)}, f32[64,256]{1,0:T(8,128)S(1)}, u32[]{:S(2)}, u32[]{:S(2)}) collective-permute-start(f32[64,256]{1,0:T(8,128)S(1)} %get-tuple-element.59), channel_id=1, source_target_pairs={{0,1},{1,0},{2,3},{3,2},{4,5},{5,4},{6,7},{7,6},{8,9},{9,8},{10,11... | collective-permute-start | bytes 196616 | tf_op jit(solution)/shard_map/ppermute | solution.py:294
  173.4 1.5 collective-permute-start.15
  175.0 1.2 copy-start.2
  176.1 4.8 %copy-start.9 = (bf16[640,512]{1,0:T(8,128)(2,1)S(1)}, bf16[640,512]{1,0:T(8,128)(2,1)}, u32[]{:S(2)}) copy-start(bf16[640,512]{1,0:T(8,128)(2,1)} %copy-done.7) | copy-start | bytes 1966084
  179.8 14.9 %collective-permute-start.16 = (f32[128,512]{1,0:T(8,128)S(1)}, f32[128,512]{1,0:T(8,128)S(1)}, u32[]{:S(2)}, u32[]{:S(2)}) collective-permute-start(f32[128,512]{1,0:T(8,128)S(1)} %get-tuple-element.57), channel_id=1, source_target_pairs={{0,8},{2,10},{4,12},{6,14},{8,0},{10,2},{12,4},{14,6},{1,9},{3,11}... | collective-permute-start | bytes 786440 | tf_op jit(solution)/shard_map/ppermute | solution.py:198

commit v2 on v1

--- a/solution.py
+++ b/solution.py
@@ -12,7 +12,7 @@
 PAIR = 2 * LAG
 
 SWAP = [(0, 1), (1, 0)]
-LIMIT = 24 << 20
+LIMIT = 20 << 20
 
 VMEM = pl.BlockSpec(memory_space=pltpu.VMEM)
 SMEM = pl.BlockSpec(memory_space=pltpu.SMEM)
@@ -43,7 +43,7 @@
             pairs[:comps, pl.ds(aligned(at + half), half)] = second[e]
             return 0
 
-        lax.fori_loop(0, blocks, one, 0)
+        lax.fori_loop(0, blocks, one, 0, unroll=blocks <= 8)
 
     @pl.when(core == 0)
     def _():
@@ -59,7 +59,7 @@
         pairs[comps:, pl.ds(aligned(at), width)] = wide[:, PAIR - LAG : PAIR - LAG + width]
         return 0
 
-    lax.fori_loop(0, blocks, shift, 0)
+    lax.fori_loop(0, blocks, shift, 0, unroll=blocks <= 8)
 
 
 def lagged_tile(pairs, start, width, count):
@@ -178,6 +178,27 @@
     ).astype(jnp.bfloat16)
 
 
+def final_kernel(scale, early, before, w, rate, kept, taken, out, held, sem):
+    del before
+    rates = jnp.concatenate([rate[...]] * (w.shape[1] // rate.shape[1]), 1)
+    grad = scale * (kept[...] + taken[...])
+    held[...] = jnp.maximum(w[early:, :].astype(jnp.float32) - rates * grad, 0.0).astype(
+        jnp.bfloat16
+    )
+    copy = pltpu.make_async_copy(held, out.at[early:, :], sem)
+    copy.start()
+    copy.wait()
+
+
+def update_kernel(scale, pieces, old, rate, new, copies):
+    grad = scale * jnp.sum(pieces[...], 0)
+    value = jnp.maximum(old[...] - rate[...] * grad, 0.0)
+    new[...] = value
+    rounded = value.astype(jnp.bfloat16)
+    for i in range(copies.shape[0]):
+        copies[i] = rounded
+
+
 def cost(rows, lagrows, scans):
     return pl.CostEstimate(
         flops=4 * rows * lagrows * scans, bytes_accessed=2 * rows * scans, transcendentals=0
@@ -196,11 +217,6 @@
 
 def sent(x, count, k):
     return lax.ppermute(x, "scan", [(i, i ^ k) for i in range(count)])
-
-
-def gathered(x, count):
-    copies = jnp.broadcast_to(x[None], (count,) + x.shape)
-    return lax.all_to_all(copies, "scan", 0, 0, tiled=True)
 
 
 def per_device(spectra, templates, activations, h_rate, w_rate):
@@ -220,20 +236,20 @@
         return me ^ jnp.array(ks, jnp.int32)
 
     own = templates.reshape(rows, lagrows)
-    act_half = lax.dynamic_slice(activations, (0, core * half), (comps, half))
     across = count // 2
     late = late_rows(rows)
     early = rows - late
 
+    act_half = lax.dynamic_slice(activations, (0, core * half), (comps, half))
     rounded = act_half.astype(jnp.bfloat16)
     even = list(range(0, count, 2))
     blocks = spectra.reshape(count, rows, width)
     order = send_order(count)
     landed = {}
-    block = rounded
     for i, k in enumerate(order + [0]):
-        place, block, rounded = lax.optimization_barrier((me ^ k, block, rounded))
+        place = me ^ k
         if i:
+            place, block = lax.optimization_barrier((place, block))
             landed[order[i - 1]] = sent(block, count, order[i - 1])
         if i == 1:
             column = jnp.stack([rounded] + [sent(rounded, count, e) for e in even[1:]])
@@ -287,9 +303,18 @@
     give, keep = sums
     both = keep + lax.ppermute(give, "mz", SWAP)
     pieces = lax.all_to_all(both, "scan", 0, 0, tiled=True)
-    grad = scale * jnp.sum(pieces, 0)
-    new_half = jnp.maximum(act_half - h_rate[:, None] * grad, 0.0)
-    mine_new = gathered(new_half.astype(jnp.bfloat16), count)
+    new_half, copies = pl.pallas_call(
+        functools.partial(update_kernel, scale),
+        out_shape=[
+            jax.ShapeDtypeStruct((comps, half), jnp.float32),
+            jax.ShapeDtypeStruct(part, jnp.bfloat16),
+        ],
+        in_specs=[VMEM] * 3,
+        out_specs=[VMEM] * 2,
+        compiler_params=pltpu.CompilerParams(vmem_limit_bytes=8 << 20),
+        name="update",
+    )(pieces, act_half, h_rate[:, None])
+    mine_new = lax.all_to_all(copies, "scan", 0, 0, tiled=True)
     other_new = lax.ppermute(mine_new, "mz", SWAP)
     new_other = lax.ppermute(new_half, "mz", SWAP)
     new_h = jnp.where(
@@ -332,11 +357,16 @@
         name="second",
     )
     new_w = second(ids(use), all_rows, w_rate[None, :], pairs_new, *[landed[k] for k in use])
-    rates = jnp.tile(w_rate, lags)[None, :]
-    new_late = own[early:].astype(jnp.float32) - rates * (scale * (kept + taken))
-    new_w = lax.dynamic_update_slice(
-        new_w, jnp.maximum(new_late, 0.0).astype(jnp.bfloat16), (early, 0)
-    )
+    new_w = pl.pallas_call(
+        functools.partial(final_kernel, scale, early),
+        out_shape=jax.ShapeDtypeStruct((rows, lagrows), jnp.bfloat16),
+        in_specs=[ANY] + [VMEM] * 4,
+        out_specs=ANY,
+        scratch_shapes=[pltpu.VMEM((late, lagrows), jnp.bfloat16), pltpu.SemaphoreType.DMA],
+        input_output_aliases={0: 0},
+        compiler_params=pltpu.CompilerParams(vmem_limit_bytes=8 << 20),
+        name="final",
+    )(new_w, own, w_rate[None, :], kept, taken)
     return (new_h, new_w.reshape(templates.shape))
 
 

time: 197 us -> 197 us (level)
  waiting for transfers between devices: 83 us -> 80.2 us
  starting transfers between devices: 47.2 us -> 44.6 us
  other arithmetic: 8.67 us -> 10.8 us
    ppermute x13, starting transfers between devices: 26 us -> 22.9 us  [sent(): return lax.ppermute(x, 'scan', [(i, i ^ k) for i in range(count)])]
    unnamed x42 -> x47, local copies, waits for them, and re-layouts: 7.17 us -> 10 us
    ppermute x13, waiting for transfers between devices: 56.6 us -> 53.7 us  [sent(): return lax.ppermute(x, 'scan', [(i, i ^ k) for i in range(count)])]
    concatenate x4, other arithmetic: 3.09 us -> 5.07 us  [per_device(): block = jnp.concatenate([block, extra], 0)]
  transfers between devices with their start and end apart: 19 -> 19, of which waited for: 11 -> 10; matrix products, arithmetic and copies ran while one was open for 12% -> 15% of each run, Pallas kernels for 12% -> 12%
where the time goes in v2:
time: 197 us; the launch traced here: 196 us
  waiting for transfers between devices  80.2 us (41%)
  starting transfers between devices  44.6 us (23%)
  Pallas kernels  30 us (15%)
  local copies, waits for them, and re-layouts  29.4 us (15%)
  other arithmetic  10.8 us (5%)
    ppermute x13, waiting for transfers between devices, sent(): return lax.ppermute(x, 'scan', [(i, i ^ k) for i in range(count)])  53.7 us
    ppermute x13, starting transfers between devices, sent(): return lax.ppermute(x, 'scan', [(i, i ^ k) for i in range(count)])  22.9 us
    all_to_all x1, starting transfers between devices, per_device(): pieces = lax.all_to_all(both, 'scan', 0, 0, tiled=True)  17.9 us
    pallas_call x4, Pallas kernels, per_device(): sums = call(core_id, ids(ks), all_rows, all_rows_t, pairs, *sums, *data)  15.1 us
    all_to_all x1, waiting for transfers between devices, per_device(): pieces = lax.all_to_all(both, 'scan', 0, 0, tiled=True)  14.7 us
    unnamed x47, local copies, waits for them, and re-layouts  10 us
    pallas_call x1, Pallas kernels, per_device(): second(ids(use), all_rows, w_rate[None, :], pairs_new, *[landed[k] for k...  9.41 us
    all_to_all x1, waiting for transfers between devices, per_device(): mine_new = lax.all_to_all(copies, 'scan', 0, 0, tiled=True)  9 us
  transfers between devices with their start and end apart: 19, of which 10 were waited for; matrix products, arithmetic and copies ran while one was open for 15% of the time, Pallas kernels for 12%

profile of v2, /device:TPU:0, one launch (start us, length us, event | category | flops | bytes accessed | tf_op | source)
XLA Modules:
  0.0 196.0 jit_solution(198810096464258450)
XLA Ops:
  0.6 1.5 constant_dynamic-update-slice_fusion.4
  2.1 3.1 %collective-permute-start.1 = (bf16[64,256]{1,0:T(8,128)(2,1)S(1)}, bf16[64,256]{1,0:T(8,128)(2,1)S(1)}, u32[]{:S(2)}, u32[]{:S(2)}) collective-permute-start(bf16[64,256]{1,0:T(8,128)(2,1)S(1)} %get-tuple-element.57), channel_id=1, source_target_pairs={{0,4},{2,6},{4,0},{6,2},{8,12},{10,14},{12,8},{14,10},{1,5},{3,7},... | collective-permute-start | bytes 98312 | tf_op jit(solution)/shard_map/ppermute | solution.py:219
  5.2 2.6 %collective-permute-start.2 = (bf16[64,256]{1,0:T(8,128)(2,1)S(1)}, bf16[64,256]{1,0:T(8,128)(2,1)S(1)}, u32[]{:S(2)}, u32[]{:S(2)}) collective-permute-start(bf16[64,256]{1,0:T(8,128)(2,1)S(1)} %get-tuple-element.57), channel_id=1, source_target_pairs={{0,8},{2,10},{4,12},{6,14},{8,0},{10,2},{12,4},{14,6},{1,9},{3,11}... | collective-permute-start | bytes 98312 | tf_op jit(solution)/shard_map/ppermute | solution.py:219
  7.8 1.1 dynamic-slice_bitcast_fusion.7
  8.9 1.2 dynamic-slice_bitcast_fusion.3
  10.1 0.9 dynamic-slice_bitcast_fusion.11
  11.0 1.0 pad_maximum_fusion.1
  12.0 0.9 collective-permute-start.7
  12.9 3.5 %collective-permute-start.6 = (bf16[640,512]{1,0:T(8,128)(2,1)S(1)}, bf16[640,512]{1,0:T(8,128)(2,1)S(1)}, u32[]{:S(2)}, u32[]{:S(2)}) collective-permute-start(bf16[640,512]{1,0:T(8,128)(2,1)S(1)} %dynamic-slice_bitcast_fusion.7), channel_id=1, source_target_pairs={{0,8},{2,10},{4,12},{6,14},{8,0},{10,2},{12,4},{14,6},{1,9},{3,11}... | collective-permute-start | bytes 1966088 | tf_op jit(solution)/shard_map/ppermute | solution.py:219
  16.4 1.9 dynamic-slice_bitcast_fusion.6
  18.3 1.2 dynamic-slice_bitcast_fusion.2
  19.5 0.9 dynamic-slice_bitcast_fusion.10
  20.5 1.0 pad_maximum_fusion.2
  21.5 2.1 %dynamic-slice_bitcast_fusion.5 = bf16[640,512]{1,0:T(8,128)(2,1)} fusion(bf16[8,768,512]{2,1,0:T(8,128)(2,1)} %bitcast.53, s32[]{:T(128)S(6)} %select_n.56), kind=kLoop, calls=%fused_computation.10 | loop fusion | bytes 1310724 | tf_op jit(solution)/shard_map/squeeze | solution.py:258
  23.5 2.1 %dynamic-slice_bitcast_fusion.1 = bf16[768,512]{1,0:T(8,128)(2,1)} fusion(bf16[8,768,512]{2,1,0:T(8,128)(2,1)} %bitcast.54, s32[]{:T(128)S(6)} %select_n.57), kind=kLoop, calls=%fused_computation.6 | loop fusion | bytes 1572868 | tf_op jit(solution)/shard_map/jit(dynamic_index_in_dim)/squeeze | solution.py:260
  25.6 0.9 dynamic-slice_bitcast_fusion.9
  26.6 0.7 slice_bitcast_fusion
  27.2 2.1 %pad_maximum_fusion.3 = bf16[896,512]{1,0:T(8,128)(2,1)} fusion(bf16[128,512]{1,0:T(8,128)(2,1)S(1)} %dynamic-slice_bitcast_fusion.9, bf16[768,512]{1,0:T(8,128)(2,1)} %dynamic-slice_bitcast_fusion.1), kind=kLoop, calls=%fused_computation.3 | loop fusion | flops 1835008 | bytes 1835008 | tf_op jit(solution)/shard_map/concatenate | solution.py:262
  29.4 1.7 collective-permute-start.9
  31.1 0.6 copy-done.15
  32.1 0.8 constant_dynamic-update-slice_fusion.3
  32.9 0.8 constant_dynamic-update-slice_fusion.2
  33.6 0.8 constant_dynamic-update-slice_fusion.1
  34.4 2.4 %collective-permute-done.4 = bf16[4,64,256]{2,1,0:T(8,128)(2,1)S(1)} collective-permute-done((bf16[4,64,256]{2,1,0:T(8,128)(2,1)S(1)}, bf16[4,64,256]{2,1,0:T(8,128)(2,1)S(1)}, u32[]{:S(2)}, u32[]{:S(2)}) %collective-permute-start.4) | collective-permute-done | bytes 131104 | tf_op jit(solution)/shard_map/ppermute | solution.py:219
  36.9 2.0 %dynamic-slice_bitcast_fusion.4 = bf16[640,512]{1,0:T(8,128)(2,1)} fusion(bf16[8,768,512]{2,1,0:T(8,128)(2,1)} %bitcast.56, s32[]{:T(128)S(6)} %select_n.59), kind=kLoop, calls=%fused_computation.9 | loop fusion | bytes 1310724 | tf_op jit(solution)/shard_map/squeeze | solution.py:258
  38.9 0.7 broadcast_xor_fusion.3.ids
  39.5 11.3 %collective-permute-done = bf16[128,512]{1,0:T(8,128)(2,1)} collective-permute-done((bf16[128,512]{1,0:T(8,128)(2,1)}, bf16[128,512]{1,0:T(8,128)(2,1)}, u32[]{:S(2)}, u32[]{:S(2)}) %collective-permute-start) | collective-permute-done | bytes 131104 | tf_op jit(solution)/shard_map/ppermute | solution.py:219
  50.8 4.3 %collective-permute-start.8 = (bf16[640,512]{1,0:T(8,128)(2,1)}, bf16[640,512]{1,0:T(8,128)(2,1)}, u32[]{:S(2)}, u32[]{:S(2)}) collective-permute-start(bf16[640,512]{1,0:T(8,128)(2,1)} %dynamic-slice_bitcast_fusion.6), channel_id=1, source_target_pairs={{0,10},{2,8},{4,14},{6,12},{8,2},{10,0},{12,6},{14,4},{1,11},{3,9}... | collective-permute-start | bytes 1966088 | tf_op jit(solution)/shard_map/ppermute | solution.py:219
  55.7 1.6 dynamic-slice_bitcast_fusion.8
  57.2 1.2 dynamic-slice_bitcast_fusion
  58.4 0.8 copy-done.10
  59.3 2.9 %collective-permute-start.10 = (bf16[640,512]{1,0:T(8,128)(2,1)}, bf16[640,512]{1,0:T(8,128)(2,1)}, u32[]{:S(2)}, u32[]{:S(2)}) collective-permute-start(bf16[640,512]{1,0:T(8,128)(2,1)} %dynamic-slice_bitcast_fusion.5), channel_id=1, source_target_pairs={{0,12},{2,14},{4,8},{6,10},{8,4},{10,6},{12,0},{14,2},{1,13},{3,15... | collective-permute-start | bytes 1966088 | tf_op jit(solution)/shard_map/ppermute | solution.py:219
  62.2 1.0 pad_maximum_fusion.4.rest_0_
  63.2 0.9 copy-done.1
  64.1 1.9 collective-permute-start.12
  66.0 2.0 %fusion = (bf16[512,896]{0,1:T(8,128)(2,1)}, bf16[896,512]{1,0:T(8,128)(2,1)S(1)}) fusion(bf16[128,512]{1,0:T(8,128)(2,1)} %collective-permute-done, bf16[768,512]{1,0:T(8,128)(2,1)S(1)} %bitcast.43), kind=kLoop, calls=%fused_computation.32 | loop fusion | flops 1835008 | bytes 2752512 | tf_op jit(solution)/shard_map/transpose | solution.py:267
  68.0 1.5 copy.18.wt
  69.5 0.9 copy-done.5
  70.5 0.9 copy-done.8
  71.4 0.9 stack.21.pairs
  72.3 1.2 copy-done.2
  73.4 1.1 copy-done.11
  74.5 4.5 %first.4 = (f32[8,64,256]{2,1,0:T(8,128)S(1)}, f32[8,64,256]{2,1,0:T(8,128)S(1)}) custom-call(s32[1]{0:T(128)} %bitcast.core, s32[3]{0:T(128)S(1)} %broadcast_xor_fusion.1.ids, bf16[896,512]{1,0:T(8,128)(2,1)S(1)} %get-tuple-element.60.w, bf16[512,896]{1,0:T(8,128)(2,1)S(1)} %copy.18.wt, bf16[128,4608]{1,0:T(8,128)(2,1)S(1)} %stack.21.pairs, ...), custom_call_target="tpu_custom_call" | custom-call | flops 2415919104 | bytes 2359296 | tf_op jit(solution)/shard_map/first/pallas_call | solution.py:301
  79.1 6.3 %collective-permute-done.8.rest_2_.rest_3_ = bf16[640,512]{1,0:T(8,128)(2,1)} collective-permute-done((bf16[640,512]{1,0:T(8,128)(2,1)}, bf16[640,512]{1,0:T(8,128)(2,1)}, u32[]{:S(2)}, u32[]{:S(2)}) %collective-permute-start.8) | collective-permute-done | bytes 655392 | tf_op jit(solution)/shard_map/ppermute | solution.py:219
  85.4 4.1 %first.5 = (f32[8,64,256]{2,1,0:T(8,128)S(1)}, f32[8,64,256]{2,1,0:T(8,128)S(1)}) custom-call(s32[1]{0:T(128)} %bitcast.core, s32[2]{0:T(128)S(1)} %broadcast_xor_fusion.2.ids, bf16[896,512]{1,0:T(8,128)(2,1)S(1)} %get-tuple-element.60.w, bf16[512,896]{1,0:T(8,128)(2,1)S(1)} %copy.18.wt, bf16[128,4608]{1,0:T(8,128)(2,1)S(1)} %stack.21.pairs, ...), custom_call_target="tpu_custom_call" | custom-call | flops 1610612736 | bytes 1572864 | tf_op jit(solution)/shard_map/first/pallas_call | solution.py:301
  89.5 12.7 %collective-permute-done.10.rest_2_.rest_5_ = bf16[640,512]{1,0:T(8,128)(2,1)} collective-permute-done((bf16[640,512]{1,0:T(8,128)(2,1)}, bf16[640,512]{1,0:T(8,128)(2,1)}, u32[]{:S(2)}, u32[]{:S(2)}) %collective-permute-start.10) | collective-permute-done | bytes 655392 | tf_op jit(solution)/shard_map/ppermute | solution.py:219
  102.2 16.7 %collective-permute-done.11.rest_3_.rest_6_ = bf16[896,512]{1,0:T(8,128)(2,1)} collective-permute-done((bf16[896,512]{1,0:T(8,128)(2,1)}, bf16[896,512]{1,0:T(8,128)(2,1)}, u32[]{:S(2)}, u32[]{:S(2)}) %collective-permute-start.11) | collective-permute-done | bytes 917536 | tf_op jit(solution)/shard_map/ppermute | solution.py:219
  118.9 4.1 %first.6 = (f32[8,64,256]{2,1,0:T(8,128)S(1)}, f32[8,64,256]{2,1,0:T(8,128)S(1)}) custom-call(s32[1]{0:T(128)} %bitcast.core, s32[2]{0:T(128)S(1)} %broadcast_xor_fusion.3.ids, bf16[896,512]{1,0:T(8,128)(2,1)S(1)} %get-tuple-element.60.w, bf16[512,896]{1,0:T(8,128)(2,1)S(1)} %copy.18.wt, bf16[128,4608]{1,0:T(8,128)(2,1)S(1)} %stack.21.pairs, ...), custom_call_target="tpu_custom_call" | custom-call | flops 1610612736 | bytes 1572864 | tf_op jit(solution)/shard_map/first/pallas_call | solution.py:301
  123.0 2.4 %first.7 = (f32[8,64,256]{2,1,0:T(8,128)S(1)}, f32[8,64,256]{2,1,0:T(8,128)S(1)}) custom-call(s32[1]{0:T(128)} %bitcast.core, s32[1]{0:T(128)} %bitcast.1.ids, bf16[896,512]{1,0:T(8,128)(2,1)S(1)} %get-tuple-element.60.w, bf16[512,896]{1,0:T(8,128)(2,1)S(1)} %copy.18.wt, bf16[128,4608]{1,0:T(8,128)(2,1)S(1)} %stack.21.pairs, ...), custom_call_target="tpu_custom_call" | custom-call | flops 805306368 | bytes 786432 | tf_op jit(solution)/shard_map/first/pallas_call | solution.py:301
  125.4 1.9 collective-permute-done.13
  127.3 0.9 add.56
  128.3 17.9 %all-to-all-start = ((f32[8,64,256]{2,1,0:T(8,128)}), f32[8,64,256]{2,1,0:T(8,128)S(1)}, u32[]{:S(2)}, u32[]{:S(2)}) async-start(f32[8,64,256]{2,1,0:T(8,128)} %add.56), calls=%async_computation | async-start | bytes 1048576 | tf_op jit(solution)/shard_map/all_to_all | solution.py:305
  146.2 14.7 %all-to-all-done.pieces = f32[8,64,256]{2,1,0:T(8,128)S(1)} async-done(((f32[8,64,256]{2,1,0:T(8,128)}), f32[8,64,256]{2,1,0:T(8,128)S(1)}, u32[]{:S(2)}, u32[]{:S(2)}) %all-to-all-start) | async-done | bytes 524320 | tf_op jit(solution)/shard_map/all_to_all | solution.py:305
  160.9 0.8 update.1
  161.8 3.6 %all-to-all-start.1 = ((bf16[8,64,256]{2,1,0:T(8,128)(2,1)}), bf16[8,64,256]{2,1,0:T(8,128)(2,1)S(1)}, u32[]{:S(2)}, u32[]{:S(2)}) async-start(bf16[8,64,256]{2,1,0:T(8,128)(2,1)} %get-tuple-element.52), calls=%async_computation.1 | async-start | bytes 524288 | tf_op jit(solution)/shard_map/all_to_all | solution.py:317
  165.5 9.0 %all-to-all-done.1.mine = bf16[8,64,256]{2,1,0:T(8,128)(2,1)S(1)} async-done(((bf16[8,64,256]{2,1,0:T(8,128)(2,1)}), bf16[8,64,256]{2,1,0:T(8,128)(2,1)S(1)}, u32[]{:S(2)}, u32[]{:S(2)}) %all-to-all-start.1) | async-done | bytes 262176 | tf_op jit(solution)/shard_map/all_to_all | solution.py:317
  174.5 0.7 maximum_select_fusion
  175.2 0.8 collective-permute-done.15.other
  176.0 1.2 copy-done.3
  177.2 3.1 %late.1 = (bf16[128,4608]{1,0:T(8,128)(2,1)S(1)}, f32[128,512]{1,0:T(8,128)S(1)}, f32[128,512]{1,0:T(8,128)S(1)}) custom-call(s32[1]{0:T(128)} %bitcast.core, s32[4]{0:T(128)S(1)} %broadcast_xor_fusion.ids, bf16[896,512]{1,0:T(8,128)(2,1)S(1)} %get-tuple-element.60.w, bf16[8,64,256]{2,1,0:T(8,128)(2,1)S(1)} %all-to-all-done.1.mine, ...), custom_call_target="tpu_custom_call" | custom-call | flops 1073741824 | bytes 1048576 | tf_op jit(solution)/shard_map/late/pallas_call | solution.py:328
  180.3 1.1 collective-permute-start.16
  181.4 9.4 %second.1.before = bf16[768,512]{1,0:T(8,128)(2,1)} custom-call(s32[8]{0:T(128)S(1)} %broadcast_xor_fusion.4.ids, bf16[896,512]{1,0:T(8,128)(2,1)S(1)} %get-tuple-element.60.w, f32[1,64]{1,0:T(1,128)S(1)} %bitcast.45, bf16[128,4608]{1,0:T(8,128)(2,1)S(1)} %get-tuple-element.53.pairs, bf16[896,512]{1,0:T(8,128)(2,1)S(1)} %pad_maximum_fusion.4.rest_0_, ...), custom_call_target="tpu_custom_call" | custom-call | flops 5368709120 | bytes 5242880 | tf_op jit(solution)/shard_map/second/pallas_call | solution.py:359
  190.8 4.4 %collective-permute-done.16.taken = f32[128,512]{1,0:T(8,128)S(1)} collective-permute-done((f32[128,512]{1,0:T(8,128)S(1)}, f32[128,512]{1,0:T(8,128)S(1)}, u32[]{:S(2)}, u32[]{:S(2)}) %collective-permute-start.16) | collective-permute-done | bytes 262176 | tf_op jit(solution)/shard_map/ppermute | solution.py:219
  195.2 0.8 final.1
  (61 shorter events, 1.3 us)
Async XLA Ops:
  2.1 27.3 %collective-permute-start.1 = (bf16[64,256]{1,0:T(8,128)(2,1)S(1)}, bf16[64,256]{1,0:T(8,128)(2,1)S(1)}, u32[]{:S(2)}, u32[]{:S(2)}) collective-permute-start(bf16[64,256]{1,0:T(8,128)(2,1)S(1)} %get-tuple-element.57), channel_id=1, source_target_pairs={{0,4},{2,6},{4,0},{6,2},{8,12},{10,14},{12,8},{14,10},{1,5},{3,7},... | collective-permute-start | bytes 98312 | tf_op jit(solution)/shard_map/ppermute | solution.py:219
  5.2 24.2 %collective-permute-start.2 = (bf16[64,256]{1,0:T(8,128)(2,1)S(1)}, bf16[64,256]{1,0:T(8,128)(2,1)S(1)}, u32[]{:S(2)}, u32[]{:S(2)}) collective-permute-start(bf16[64,256]{1,0:T(8,128)(2,1)S(1)} %get-tuple-element.57), channel_id=1, source_target_pairs={{0,8},{2,10},{4,12},{6,14},{8,0},{10,2},{12,4},{14,6},{1,9},{3,11}... | collective-permute-start | bytes 98312 | tf_op jit(solution)/shard_map/ppermute | solution.py:219
  7.8 23.4 %collective-permute-start.3 = (bf16[64,256]{1,0:T(8,128)(2,1)S(1)}, bf16[64,256]{1,0:T(8,128)(2,1)S(1)}, u32[]{:S(2)}, u32[]{:S(2)}) collective-permute-start(bf16[64,256]{1,0:T(8,128)(2,1)S(1)} %get-tuple-element.57), channel_id=1, source_target_pairs={{0,12},{2,14},{4,8},{6,10},{8,4},{10,6},{12,0},{14,2},{1,13},{3,15... | collective-permute-start | bytes 98312 | tf_op jit(solution)/shard_map/ppermute | solution.py:219
  12.0 51.2 %collective-permute-start.7 = (bf16[896,512]{1,0:T(8,128)(2,1)}, bf16[896,512]{1,0:T(8,128)(2,1)S(1)}, u32[]{:S(2)}, u32[]{:S(2)}) collective-permute-start(bf16[896,512]{1,0:T(8,128)(2,1)} %pad_maximum_fusion.1), channel_id=1, source_target_pairs={{0,4},{2,6},{4,0},{6,2},{8,12},{10,14},{12,8},{14,10},{1,5},{3,7},... | collective-permute-start | bytes 2752520 | tf_op jit(solution)/shard_map/ppermute | solution.py:219
  12.9 45.5 %collective-permute-start.6 = (bf16[640,512]{1,0:T(8,128)(2,1)S(1)}, bf16[640,512]{1,0:T(8,128)(2,1)S(1)}, u32[]{:S(2)}, u32[]{:S(2)}) collective-permute-start(bf16[640,512]{1,0:T(8,128)(2,1)S(1)} %dynamic-slice_bitcast_fusion.7), channel_id=1, source_target_pairs={{0,8},{2,10},{4,12},{6,14},{8,0},{10,2},{12,4},{14,6},{1,9},{3,11}... | collective-permute-start | bytes 1966088 | tf_op jit(solution)/shard_map/ppermute | solution.py:219
  21.4 5.1 %copy-start.21 = (s32[8]{0:T(128)S(1)}, s32[8]{0:T(128)}, u32[]{:S(2)}) copy-start(s32[8]{0:T(128)} %constant.56.clone) | copy-start | bytes 100
  21.4 5.1 %copy-start.20 = (s32[3]{0:T(128)S(1)}, s32[3]{0:T(128)}, u32[]{:S(2)}) copy-start(s32[3]{0:T(128)} %constant.57.clone) | copy-start | bytes 40
  21.4 5.1 %copy-start = (bf16[1,768,512]{2,1,0:T(8,128)(2,1)S(1)}, bf16[1,768,512]{2,1,0:T(8,128)(2,1)}, u32[]{:S(2)}) copy-start(bf16[1,768,512]{2,1,0:T(8,128)(2,1)} %param.13) | copy-start | bytes 2359300
  21.5 5.8 %copy-start.19 = (s32[2]{0:T(128)S(1)}, s32[2]{0:T(128)}, u32[]{:S(2)}) copy-start(s32[2]{0:T(128)} %constant.58.clone) | copy-start | bytes 28
  29.4 1.8 copy-start.13
  29.4 21.4 %collective-permute-start = (bf16[128,512]{1,0:T(8,128)(2,1)}, bf16[128,512]{1,0:T(8,128)(2,1)}, u32[]{:S(2)}, u32[]{:S(2)}) collective-permute-start(bf16[128,512]{1,0:T(8,128)(2,1)} %slice_bitcast_fusion), channel_id=1, source_target_pairs={{0,8},{2,10},{4,12},{6,14},{8,0},{10,2},{12,4},{14,6},{1,9},{3,11}... | collective-permute-start | bytes 393224 | tf_op jit(solution)/shard_map/ppermute | solution.py:219
  29.4 1.7 copy-start.14
  29.4 56.0 %collective-permute-start.9 = (bf16[896,512]{1,0:T(8,128)(2,1)}, bf16[896,512]{1,0:T(8,128)(2,1)}, u32[]{:S(2)}, u32[]{:S(2)}) collective-permute-start(bf16[896,512]{1,0:T(8,128)(2,1)} %pad_maximum_fusion.2), channel_id=1, source_target_pairs={{0,6},{2,4},{4,2},{6,0},{8,14},{10,12},{12,10},{14,8},{1,7},{3,5},... | collective-permute-start | bytes 2752520 | tf_op jit(solution)/shard_map/ppermute | solution.py:219
  31.1 0.6 copy-start.15
  31.8 5.0 %collective-permute-start.4 = (bf16[4,64,256]{2,1,0:T(8,128)(2,1)S(1)}, bf16[4,64,256]{2,1,0:T(8,128)(2,1)S(1)}, u32[]{:S(2)}, u32[]{:S(2)}) collective-permute-start(bf16[4,64,256]{2,1,0:T(8,128)(2,1)S(1)} %pad_maximum_fusion.5), channel_id=1, source_target_pairs={{0,2},{2,0},{4,6},{6,4},{8,10},{10,8},{12,14},{14,12},{1,3},{3,1},... | collective-permute-start | bytes 393224 | tf_op jit(solution)/shard_map/ppermute | solution.py:219
  36.8 26.4 %copy-start.4 = (bf16[8,64,256]{2,1,0:T(8,128)(2,1)}, bf16[8,64,256]{2,1,0:T(8,128)(2,1)S(1)}, u32[]{:S(2)}) copy-start(bf16[8,64,256]{2,1,0:T(8,128)(2,1)S(1)} %constant_dynamic-update-slice_fusion.mine) | copy-start | bytes 786436
  36.8 18.3 %collective-permute-start.5 = (bf16[8,64,256]{2,1,0:T(8,128)(2,1)S(1)}, bf16[8,64,256]{2,1,0:T(8,128)(2,1)S(1)}, u32[]{:S(2)}, u32[]{:S(2)}) collective-permute-start(bf16[8,64,256]{2,1,0:T(8,128)(2,1)S(1)} %constant_dynamic-update-slice_fusion.mine), channel_id=1, source_target_pairs={{0,1},{1,0},{2,3},{3,2},{4,5},{5,4},{6,7},{7,6},{8,9},{9,8},{10,11... | collective-permute-start | bytes 786440 | tf_op jit(solution)/shard_map/ppermute | solution.py:270
  50.8 34.5 %collective-permute-start.8 = (bf16[640,512]{1,0:T(8,128)(2,1)}, bf16[640,512]{1,0:T(8,128)(2,1)}, u32[]{:S(2)}, u32[]{:S(2)}) collective-permute-start(bf16[640,512]{1,0:T(8,128)(2,1)} %dynamic-slice_bitcast_fusion.6), channel_id=1, source_target_pairs={{0,10},{2,8},{4,14},{6,12},{8,2},{10,0},{12,6},{14,4},{1,11},{3,9}... | collective-permute-start | bytes 1966088 | tf_op jit(solution)/shard_map/ppermute | solution.py:219
  55.2 8.0 %copy-start.7 = (bf16[8,64,256]{2,1,0:T(8,128)(2,1)}, bf16[8,64,256]{2,1,0:T(8,128)(2,1)S(1)}, u32[]{:S(2)}) copy-start(bf16[8,64,256]{2,1,0:T(8,128)(2,1)S(1)} %collective-permute-done.5.other) | copy-start | bytes 786436
  55.2 63.7 %collective-permute-start.11 = (bf16[896,512]{1,0:T(8,128)(2,1)}, bf16[896,512]{1,0:T(8,128)(2,1)}, u32[]{:S(2)}, u32[]{:S(2)}) collective-permute-start(bf16[896,512]{1,0:T(8,128)(2,1)} %pad_maximum_fusion.3), channel_id=1, source_target_pairs={{0,2},{2,0},{4,6},{6,4},{8,10},{10,8},{12,14},{14,12},{1,3},{3,1},... | collective-permute-start | bytes 2752520 | tf_op jit(solution)/shard_map/ppermute | solution.py:219
  58.4 0.8 copy-start.10
  59.3 42.9 %collective-permute-start.10 = (bf16[640,512]{1,0:T(8,128)(2,1)}, bf16[640,512]{1,0:T(8,128)(2,1)}, u32[]{:S(2)}, u32[]{:S(2)}) collective-permute-start(bf16[640,512]{1,0:T(8,128)(2,1)} %dynamic-slice_bitcast_fusion.5), channel_id=1, source_target_pairs={{0,12},{2,14},{4,8},{6,10},{8,4},{10,6},{12,0},{14,2},{1,13},{3,15... | collective-permute-start | bytes 1966088 | tf_op jit(solution)/shard_map/ppermute | solution.py:219
  63.2 0.9 copy-start.1
  64.1 58.9 %collective-permute-start.12 = (bf16[640,512]{1,0:T(8,128)(2,1)}, bf16[640,512]{1,0:T(8,128)(2,1)}, u32[]{:S(2)}, u32[]{:S(2)}) collective-permute-start(bf16[640,512]{1,0:T(8,128)(2,1)} %dynamic-slice_bitcast_fusion.4), channel_id=1, source_target_pairs={{0,14},{2,12},{4,10},{6,8},{8,6},{10,4},{12,2},{14,0},{1,15},{3,13... | collective-permute-start | bytes 1966088 | tf_op jit(solution)/shard_map/ppermute | solution.py:219
  69.5 1.0 copy-start.5
  70.5 0.9 copy-start.8
  72.3 1.2 copy-start.2
  73.4 1.1 copy-start.11
  125.3 20.8 %copy-start.16 = (f32[64]{0:T(128)S(1)}, f32[64]{0:T(128)}, u32[]{:S(2)}) copy-start(f32[64]{0:T(128)} %param.15) | copy-start | bytes 772
  125.4 35.6 %copy-start.6 = (f32[64,256]{1,0:T(8,128)S(1)}, f32[64,256]{1,0:T(8,128)}, u32[]{:S(2)}) copy-start(f32[64,256]{1,0:T(8,128)} %get-tuple-element.58.old) | copy-start | bytes 196612
  125.4 2.0 %collective-permute-start.13 = (f32[8,64,256]{2,1,0:T(8,128)S(1)}, f32[8,64,256]{2,1,0:T(8,128)S(1)}, u32[]{:S(2)}, u32[]{:S(2)}) collective-permute-start(f32[8,64,256]{2,1,0:T(8,128)S(1)} %get-tuple-element.50), channel_id=1, source_target_pairs={{0,1},{1,0},{2,3},{3,2},{4,5},{5,4},{6,7},{7,6},{8,9},{9,8},{10,11... | collective-permute-start | bytes 1572872 | tf_op jit(solution)/shard_map/ppermute | solution.py:304
  127.3 38.0 %copy-start.18 = (s32[4]{0:T(128)S(1)}, s32[4]{0:T(128)}, u32[]{:S(2)}) copy-start(s32[4]{0:T(128)} %constant.61.clone) | copy-start | bytes 52
  127.3 47.1 %copy-start.17 = (s32[8]{0:T(128)S(1)}, s32[8]{0:T(128)}, u32[]{:S(2)}) copy-start(s32[8]{0:T(128)} %constant.62.clone) | copy-start | bytes 100
  128.3 32.7 %all-to-all-start = ((f32[8,64,256]{2,1,0:T(8,128)}), f32[8,64,256]{2,1,0:T(8,128)S(1)}, u32[]{:S(2)}, u32[]{:S(2)}) async-start(f32[8,64,256]{2,1,0:T(8,128)} %add.56), calls=%async_computation | async-start | bytes 1048576 | tf_op jit(solution)/shard_map/all_to_all | solution.py:305
  161.8 12.7 %all-to-all-start.1 = ((bf16[8,64,256]{2,1,0:T(8,128)(2,1)}), bf16[8,64,256]{2,1,0:T(8,128)(2,1)S(1)}, u32[]{:S(2)}, u32[]{:S(2)}) async-start(bf16[8,64,256]{2,1,0:T(8,128)(2,1)} %get-tuple-element.52), calls=%async_computation.1 | async-start | bytes 524288 | tf_op jit(solution)/shard_map/all_to_all | solution.py:317
  165.4 9.1 %collective-permute-start.14 = (f32[64,256]{1,0:T(8,128)S(1)}, f32[64,256]{1,0:T(8,128)S(1)}, u32[]{:S(2)}, u32[]{:S(2)}) collective-permute-start(f32[64,256]{1,0:T(8,128)S(1)} %get-tuple-element.51), channel_id=1, source_target_pairs={{0,1},{1,0},{2,3},{3,2},{4,5},{5,4},{6,7},{7,6},{8,9},{9,8},{10,11... | collective-permute-start | bytes 196616 | tf_op jit(solution)/shard_map/ppermute | solution.py:319
  174.5 1.5 collective-permute-start.15
  176.0 1.2 copy-start.3
  177.2 4.2 %copy-start.9 = (f32[64]{0:T(128)S(1)}, f32[64]{0:T(128)}, u32[]{:S(2)}) copy-start(f32[64]{0:T(128)} %param.16) | copy-start | bytes 772
  177.2 4.2 %copy-start.12 = (bf16[640,512]{1,0:T(8,128)(2,1)S(1)}, bf16[640,512]{1,0:T(8,128)(2,1)}, u32[]{:S(2)}) copy-start(bf16[640,512]{1,0:T(8,128)(2,1)} %copy-done.10) | copy-start | bytes 1966084
  180.3 14.9 %collective-permute-start.16 = (f32[128,512]{1,0:T(8,128)S(1)}, f32[128,512]{1,0:T(8,128)S(1)}, u32[]{:S(2)}, u32[]{:S(2)}) collective-permute-start(f32[128,512]{1,0:T(8,128)S(1)} %get-tuple-element.55), channel_id=1, source_target_pairs={{0,8},{2,10},{4,12},{6,14},{8,0},{10,2},{12,4},{14,6},{1,9},{3,11}... | collective-permute-start | bytes 786440 | tf_op jit(solution)/shard_map/ppermute | solution.py:219
